TPU v7x, 128 devices: a whole 4x4x4 slice. The times are simulated.
128 devices in a mesh: seq: 8 (over z, core), fsdp: 16 (over y, x).
Axes of the slice: x: 4, y: 4, z: 4, core: 2. Of those that a mesh axis runs over, the one named last changes fastest.
Arguments:
- tokens: bfloat16 [2, 16384, 8192], P(None, 'fsdp', 'seq'), may hold values from -6 to 6
- keep_index: int32 [2, 5120], P(None, 'fsdp'), may hold values from 0 to 1024, as said below
- keep_count: int32 [2, 16], replicated, may hold values from 64 to 320, as said below
- block_mask: int32 [2, 16, 16], replicated, may hold values from 0 to 1, as said below
- router: bfloat16 [8192], replicated, may hold values from -0.0625 to 0.0625
- norm_gain: float32 [8192], replicated, may hold values from 0.25 to 1.75
- w_query: bfloat16 [8192, 8192], P('fsdp', 'seq'), may hold values from -3 to 3
- w_key: bfloat16 [8192, 1024], P('fsdp', 'seq'), may hold values from -0.078125 to 0.078125
- w_value: bfloat16 [8192, 1024], P('fsdp', 'seq'), may hold values from -0.0625 to 0.0625
- w_out: bfloat16 [8192, 8192], P('seq', 'fsdp'), may hold values from -0.125 to 0.125
Outputs:
- mixed: float32 [2, 16384, 8192], P(None, 'fsdp', 'seq')
Inputs may be any that keep to these rules, and one draw needn't show every extreme that they name: `keep_index`: for each sequence s and fsdp index f, entries f * 320 to f * 320 + keep_count[s, f] - 1 are distinct positions in ascending order, the rest equal 1024. `keep_count`: each count is 64 or 320; the counts of one sequence sum to 2048. `block_mask`: 1 on the diagonal, 0 above it.
All inputs are finite; a program needn't handle non-finite values.
Results may differ from a plain program's by a relative error of at most 0.006.
Values may be sent and summed in bfloat16 or wider, within the bound.
A program may use at most 128 MiB of HBM per device.

v0:
```python
import math

import jax
import jax.numpy as jnp
from jax import lax
from jax.sharding import PartitionSpec as P

HD = 128
BLK = 128


epsilon = 1e-05


def shards(
    tokens, keep_index, keep_count, block_mask, router, norm_gain, w_query, w_key, w_value, w_out
):
    fsdp_size = lax.axis_size("fsdp")
    owner_idx = lax.axis_index("fsdp")
    seq_count, tok_dev, part_width = tokens.shape
    kept_most = keep_index.shape[1]
    slot_count = kept_most // fsdp_size
    own_rows = tok_dev // 8
    block_count = block_mask.shape[1]
    starts = jnp.cumsum(keep_count, axis=1) - keep_count
    range_ends = starts + keep_count
    my_start = lax.dynamic_index_in_dim(starts, owner_idx, 1, keepdims=False)
    my_count = lax.dynamic_index_in_dim(keep_count, owner_idx, 1, keepdims=False)
    safe_index = jnp.minimum(keep_index, tok_dev - 1)
    kept_rows = jnp.take_along_axis(tokens, safe_index[:, :, None], axis=1)
    owner_ids = jnp.arange(fsdp_size, dtype=jnp.int32)[None, :, None]
    slot_ids = jnp.arange(slot_count, dtype=jnp.int32)[None, None, :]
    first_pick = jnp.mod(owner_ids - my_start[:, None, None], fsdp_size)
    pick_index = first_pick + slot_ids * fsdp_size
    usable = (pick_index < my_count[:, None, None]).reshape(seq_count, -1)
    picked_rows = jnp.take_along_axis(
        kept_rows, jnp.minimum(pick_index, kept_most - 1).reshape(seq_count, -1)[:, :, None], axis=1
    )
    send_rows = jnp.where(usable[:, :, None], picked_rows, jnp.zeros_like(picked_rows)).reshape(
        seq_count, fsdp_size, slot_count, part_width
    )
    received = lax.all_to_all(send_rows, "fsdp", split_axis=1, concat_axis=1, tiled=True)
    kept_rank = jnp.arange(own_rows, dtype=jnp.int32) * fsdp_size + owner_idx
    source = jnp.sum((range_ends[:, None, :] <= kept_rank[None, :, None]).astype(jnp.int32), axis=2)
    source_start = jnp.take_along_axis(starts, source, axis=1)
    slot_of = (kept_rank[None, :] - source_start) // fsdp_size
    flat_index = source * slot_count + slot_of
    narrow_rows = jnp.take_along_axis(
        received.reshape(seq_count, fsdp_size * slot_count, part_width),
        flat_index[:, :, None],
        axis=1,
    )
    full_rows = lax.all_gather(narrow_rows, "seq", axis=2, tiled=True)
    full_width = full_rows.shape[2]
    row_total = seq_count * own_rows
    flat_rows = full_rows.reshape(row_total, full_width)
    router_logit = jnp.dot(flat_rows, router, preferred_element_type=jnp.float32)
    gate_value = jax.nn.sigmoid(router_logit)
    wide = flat_rows.astype(jnp.float32)
    mean_square = jnp.mean(wide * wide, axis=1, keepdims=True)
    normed = (wide * lax.rsqrt(mean_square + epsilon) * norm_gain).astype(jnp.bfloat16)
    query_sum = jnp.dot(
        normed,
        lax.all_gather(w_query, "fsdp", axis=0, tiled=True),
        preferred_element_type=jnp.float32,
    )
    key_sum = jnp.dot(
        normed,
        lax.all_gather(w_key, "fsdp", axis=0, tiled=True),
        preferred_element_type=jnp.float32,
    )
    value_sum = jnp.dot(
        normed,
        lax.all_gather(w_value, "fsdp", axis=0, tiled=True),
        preferred_element_type=jnp.float32,
    )
    local_kv = key_sum.shape[1] // HD
    local_heads = query_sum.shape[1] // HD
    group_size = local_heads // local_kv
    queries = query_sum.astype(jnp.bfloat16).reshape(seq_count, own_rows, local_kv, group_size, HD)
    key_rows = key_sum.astype(jnp.bfloat16).reshape(seq_count, own_rows, local_kv * HD)
    value_rows = value_sum.astype(jnp.bfloat16).reshape(seq_count, own_rows, local_kv * HD)
    all_keys, all_values = (
        lax.all_gather(key_rows, "fsdp", axis=1, tiled=True),
        lax.all_gather(value_rows, "fsdp", axis=1, tiled=True),
    )
    keep_total = all_keys.shape[1]
    key_position = jnp.arange(keep_total, dtype=jnp.int32)
    key_rank = key_position % own_rows * fsdp_size + key_position // own_rows
    block_ids = jnp.arange(block_count, dtype=jnp.int32)
    query_onehot = (kept_rank[:, None] // BLK == block_ids[None, :]).astype(jnp.float32)
    key_onehot = (key_rank[:, None] // BLK == block_ids[None, :]).astype(jnp.float32)
    block_open = jnp.einsum(
        "qa,sab,tb->sqt", query_onehot, block_mask.astype(jnp.float32), key_onehot
    )
    allowed = (block_open > 0.5) & (key_rank[None, None, :] <= kept_rank[None, :, None])
    open_mask = allowed[:, None, None, :, :]
    key_heads = all_keys.reshape(seq_count, keep_total, local_kv, HD)
    value_heads = all_values.reshape(seq_count, keep_total, local_kv, HD)
    scores = jnp.einsum(
        "sqkgd,stkd->skgqt", queries, key_heads, preferred_element_type=jnp.float32
    ) * (1.0 / math.sqrt(HD))
    scores = jnp.where(open_mask, scores, jnp.float32(-1e30))
    row_max = jnp.max(scores, axis=4, keepdims=True)
    weights = jnp.where(open_mask, jnp.exp(scores - row_max), jnp.float32(0.0))
    totals = jnp.sum(weights, axis=4, keepdims=True)
    mixed_values = jnp.einsum(
        "skgqt,stkd->sqkgd",
        weights.astype(jnp.bfloat16),
        value_heads,
        preferred_element_type=jnp.float32,
    )
    attended = (
        (mixed_values / jnp.transpose(totals, (0, 3, 1, 2, 4)))
        .astype(jnp.bfloat16)
        .reshape(row_total, local_heads * HD)
    )
    partial_value = jnp.dot(
        attended,
        lax.all_gather(w_out, "fsdp", axis=1, tiled=True),
        preferred_element_type=jnp.float32,
    )
    summed = lax.psum_scatter(
        partial_value.reshape(seq_count, own_rows, full_width).astype(jnp.bfloat16),
        "seq",
        scatter_dimension=2,
        tiled=True,
    ).astype(jnp.float32)
    update = (gate_value.reshape(seq_count, own_rows, 1) * summed).astype(jnp.bfloat16)
    first_back = jnp.mod(owner_idx - starts, fsdp_size)[:, :, None]
    back_pick = first_back + slot_ids * fsdp_size
    back_usable = (back_pick < keep_count[:, :, None]).reshape(seq_count, -1)
    back_slot = jnp.minimum((starts[:, :, None] + back_pick) // fsdp_size, own_rows - 1)
    back_rows = jnp.take_along_axis(update, back_slot.reshape(seq_count, -1)[:, :, None], axis=1)
    back_rows = jnp.where(back_usable[:, :, None], back_rows, jnp.zeros_like(back_rows)).reshape(
        seq_count, fsdp_size, slot_count, part_width
    )
    returned = lax.all_to_all(back_rows, "fsdp", split_axis=1, concat_axis=1, tiled=True)
    kept_pos = jnp.arange(kept_most, dtype=jnp.int32)
    their_owner = jnp.mod(my_start[:, None] + kept_pos[None, :], fsdp_size)
    flat_back = jnp.clip(
        their_owner * slot_count + kept_pos[None, :] // fsdp_size, 0, fsdp_size * slot_count - 1
    )
    landed = jnp.take_along_axis(
        returned.reshape(seq_count, fsdp_size * slot_count, part_width),
        flat_back[:, :, None],
        axis=1,
    )
    landed = jnp.where(
        (kept_pos[None, :] < my_count[:, None])[:, :, None], landed, jnp.zeros_like(landed)
    )
    result = tokens.astype(jnp.float32)
    seq_ids = jnp.arange(seq_count, dtype=jnp.int32)[:, None]
    result = result.at[seq_ids, keep_index].add(landed.astype(jnp.float32), mode="drop")
    return result


def solution(mesh):
    placed = (
        P(None, "fsdp", "seq"),
        P(None, "fsdp"),
        P(),
        P(),
        P(),
        P(),
        P("fsdp", "seq"),
        P("fsdp", "seq"),
        P("fsdp", "seq"),
        P("seq", "fsdp"),
    )
    return jax.shard_map(
        shards, mesh=mesh, in_specs=placed, out_specs=P(None, "fsdp", "seq"), check_vma=False
    )
```

profile of v0, /device:TPU:26, one launch (start us, length us, event | category | flops | bytes accessed | tf_op | source)
XLA Modules:
  0.0 718.1 jit_solution(637129097657467574)
XLA Ops:
  6.5 0.9 reduce_window_sum.11
  7.4 0.7 and_select_fusion.8
  8.1 0.9 dynamic-slice_reduce_fusion
  9.1 0.1 add.433
  9.3 0.7 fusion.53
  10.0 0.7 compare_and_fusion.1
  10.9 0.1 add.450
  11.4 11.4 %gather_fusion.1 = bf16[640,1024]{1,0:T(8,128)(2,1)S(1)} fusion(bf16[2,1024,1024]{2,1,0:T(8,128)(2,1)} %param.12, s32[640]{0:T(1024)S(1)} %reshape.863), kind=kCustom, calls=%fused_computation.3 | custom fusion | bytes 2626560 | tf_op jit(solution)/shard_map/jit(take_along_axis)/gather | solution.py:30
  22.8 0.2 broadcast_select_fusion
  23.0 7.5 %gather_fusion.4 = bf16[640,1024]{1,0:T(8,128)(2,1)S(1)} fusion(bf16[2,320,1024]{2,1,0:T(8,128)(2,1)S(1)} %broadcast_select_fusion, s32[640]{0:T(1024)S(1)} %reshape.894), kind=kCustom, calls=%fused_computation.clone | custom fusion | bytes 2626560 | tf_op jit(solution)/shard_map/jit(take_along_axis)/gather | solution.py:36
  30.6 0.3 select_select_fusion.2
  30.8 2.4 copy.49
  33.2 18.4 %all-to-all-start = ((bf16[2,16,20,1024]{3,0,2,1:T(2,128)(2,1)}), bf16[2,16,20,1024]{3,0,2,1:T(2,128)(2,1)S(1)}, u32[]{:S(2)}, u32[]{:S(2)}) async-start(bf16[2,16,20,1024]{3,0,2,1:T(2,128)(2,1)} %bitcast.9), calls=%async_computation | async-start | bytes 2621440 | tf_op jit(solution)/shard_map/all_to_all | solution.py:42
  51.8 2.4 gather_fusion
  54.3 14.1 %all-to-all-done = bf16[2,16,20,1024]{3,0,2,1:T(2,128)(2,1)S(1)} async-done(((bf16[2,16,20,1024]{3,0,2,1:T(2,128)(2,1)}), bf16[2,16,20,1024]{3,0,2,1:T(2,128)(2,1)S(1)}, u32[]{:S(2)}, u32[]{:S(2)}) %all-to-all-start) | async-done | bytes 1310752 | tf_op jit(solution)/shard_map/all_to_all | solution.py:42
  68.4 0.3 copy.50
  68.8 2.8 gather_fusion.2
  71.5 0.9 broadcast_select_fusion.1
  72.5 0.7 all-gather.14.cloned.1.call-update
  73.3 0.7 all-gather.10.cloned.1.call-update
  74.0 0.5 all-gather.18.cloned.1.call-update
  74.5 0.5 all-gather.16.cloned.1.call-start
  75.1 32.1 %all-gather.8.cloned.1.call-done = bf16[2,128,8192]{2,1,0:T(8,128)(2,1)} async-done(((bf16[2,128,1024]{2,1,0:T(8,128)(2,1)}), bf16[2,128,8192]{2,1,0:T(8,128)(2,1)}) %all-gather.8.cloned.1.call-update) | async-done | bytes 4194320 | tf_op jit(solution)/shard_map/all_gather | solution.py:53
  107.2 3.3 multiply_reduce_fusion
  110.5 0.2 copy-done.1
  110.7 3.4 multiply_convert_fusion
  114.1 38.3 %all-gather.14.cloned.1.call-done = bf16[8192,128]{1,0:T(8,128)(2,1)} async-done(((bf16[512,128]{1,0:T(8,128)(2,1)}), bf16[8192,128]{1,0:T(8,128)(2,1)}) %all-gather.14.cloned.1.call-update) | async-done | bytes 2097168 | tf_op jit(solution)/shard_map/all_gather | solution.py:69
  152.3 4.7 convolution_convert_fusion.1
  157.2 41.5 %all-gather.10.cloned.1.call-done = bf16[8192,128]{1,0:T(8,128)(2,1)} async-done(((bf16[512,128]{1,0:T(8,128)(2,1)}), bf16[8192,128]{1,0:T(8,128)(2,1)}) %all-gather.10.cloned.1.call-update) | async-done | bytes 2097168 | tf_op jit(solution)/shard_map/all_gather | solution.py:74
  198.7 4.1 convolution_convert_fusion.2
  202.8 0.7 copy.51
  203.6 0.7 all-gather.20.cloned.1.call-update
  204.5 0.1 fusion.46
  204.6 0.2 broadcast_compare_fusion
  204.8 0.6 fusion.12
  205.4 1.0 copy.53
  206.4 105.0 %all-gather.18.cloned.1.call-done = bf16[8192,1024]{1,0:T(8,128)(2,1)} async-done(((bf16[512,1024]{1,0:T(8,128)(2,1)}), bf16[8192,1024]{1,0:T(8,128)(2,1)}) %all-gather.18.cloned.1.call-update) | async-done | bytes 16777232 | tf_op jit(solution)/shard_map/all_gather | solution.py:64
  311.5 11.5 %fusion.16 = bf16[32,8,8,128]{3,1,2,0:T(8,128)(2,1)S(1)} fusion(bf16[256,8192]{1,0:T(8,128)(2,1)} %multiply_convert_fusion, bf16[8192,1024]{1,0:T(8,128)(2,1)} %all-gather.18.cloned.1.call-done), kind=kOutput, calls=%fused_computation.29 | convolution fusion | flops 4295229440 | bytes 21495808 | tf_op jit(solution)/shard_map/dot_general | solution.py:62
  323.0 0.1 copy.63
  323.1 32.1 %all-gather.16.cloned.1.call-done = bf16[2,2048,128]{2,1,0:T(8,128)(2,1)} async-done(((bf16[2,128,128]{2,1,0:T(8,128)(2,1)}), bf16[2,2048,128]{2,1,0:T(8,128)(2,1)}) %all-gather.16.cloned.1.call-update) | async-done | bytes 1048592 | tf_op jit(solution)/shard_map/all_gather | solution.py:84
  355.2 3.8 fusion.2
  359.0 5.7 copy-done
  364.7 4.0 fusion.3
  368.8 30.8 %all-gather.12.cloned.1.call-done = bf16[2,2048,128]{1,2,0:T(8,128)(2,1)} async-done(((bf16[2,128,128]{1,2,0:T(8,128)(2,1)}), bf16[2,2048,128]{1,2,0:T(8,128)(2,1)}) %all-gather.12.cloned.1.call-update) | async-done | bytes 1048592 | tf_op jit(solution)/shard_map/all_gather | solution.py:85
  399.6 10.3 %divide_convert_fusion = bf16[2,128,1,8,128]{1,4,3,0,2:T(8,128)(2,1)S(1)} fusion(f32[2,2048,128,8]{2,1,3,0:T(8,128)} %copy-done, f32[2,8,128]{2,1,0:T(8,128)S(1)} %get-tuple-element.16, pred[2,128,2048]{1,2,0:T(8,128)(4,1)S(1)} %copy.53, bf16[2,2048,128]{1,2,0:T(8,128)(2,1)} %all-gather.12.cloned.1.call-done, f32[2,128,8]{1,2,0:T(8,128)S(1)} %bitcast.160), kind=kOutput, calls=%fused_computation.36 | convolution fusion | flops 1095237632 | bytes 18890752 | tf_op jit(solution)/shard_map/skgqt,stkd->sqkgd/dot_general | solution.py:107
  409.9 110.9 %all-gather.20.cloned.1.call-done = bf16[1024,8192]{1,0:T(8,128)(2,1)} async-done(((bf16[1024,512]{1,0:T(8,128)(2,1)}), bf16[1024,8192]{1,0:T(8,128)(2,1)}) %all-gather.20.cloned.1.call-update) | async-done | bytes 16777232 | tf_op jit(solution)/shard_map/all_gather | solution.py:120
  520.8 12.2 %fusion.5 = bf16[2,128,8192]{2,1,0:T(8,128)(2,1)} fusion(bf16[2,128,1024]{1,2,0:T(8,128)(2,1)S(1)} %bitcast.155, bf16[1024,8192]{1,0:T(8,128)(2,1)} %all-gather.20.cloned.1.call-done), kind=kOutput, calls=%fused_computation.14 | convolution fusion | flops 4297064448 | bytes 21495808 | tf_op jit(solution)/shard_map/dot_general | solution.py:118
  533.0 0.7 copy-done.3
  533.8 0.1 add_compare_fusion
  533.9 3.4 fusion.77
  537.3 35.0 %reduce-scatter.2.cloned.1.call-done = bf16[2,128,1024]{2,1,0:T(8,128)(2,1)} async-done(((bf16[2,128,8192]{2,1,0:T(8,128)(2,1)}), bf16[2,128,1024]{2,1,0:T(8,128)(2,1)}) %reduce-scatter.2.cloned.1.call-update) | async-done | bytes 524304 | tf_op jit(solution)/shard_map/reduce_scatter | solution.py:123
  572.4 1.2 multiply_convert_fusion.1
  573.6 7.5 %gather_fusion.3 = bf16[640,1024]{1,0:T(8,128)(2,1)S(1)} fusion(bf16[2,128,1024]{2,1,0:T(8,128)(2,1)S(1)} %multiply_convert_fusion.1, s32[640]{0:T(1024)S(1)} %reshape.875), kind=kCustom, calls=%fused_computation.5 | custom fusion | bytes 2626560 | tf_op jit(solution)/shard_map/jit(take_along_axis)/gather | solution.py:134
  581.1 0.3 gather.28
  581.4 0.3 select_select_fusion
  581.7 2.4 copy.57
  584.1 7.5 %all-to-all-start.1 = ((bf16[2,16,20,1024]{3,0,2,1:T(2,128)(2,1)}), bf16[2,16,20,1024]{3,0,2,1:T(2,128)(2,1)S(1)}, u32[]{:S(2)}, u32[]{:S(2)}) async-start(bf16[2,16,20,1024]{3,0,2,1:T(2,128)(2,1)} %copy.57), calls=%async_computation.2 | async-start | bytes 2621440 | tf_op jit(solution)/shard_map/all_to_all | solution.py:138
  591.6 6.6 convert_element_type.47
  598.6 7.3 %all-to-all-done.1 = bf16[2,16,20,1024]{3,0,2,1:T(2,128)(2,1)S(1)} async-done(((bf16[2,16,20,1024]{3,0,2,1:T(2,128)(2,1)}), bf16[2,16,20,1024]{3,0,2,1:T(2,128)(2,1)S(1)}, u32[]{:S(2)}, u32[]{:S(2)}) %all-to-all-start.1) | async-done | bytes 1310752 | tf_op jit(solution)/shard_map/all_to_all | solution.py:138
  606.0 0.3 copy.58
  606.3 7.5 %gather_fusion.5 = bf16[640,1024]{1,0:T(8,128)(2,1)S(1)} fusion(bf16[2,320,1024]{2,1,0:T(8,128)(2,1)S(1)} %copy.58, s32[640]{0:T(1024)S(1)} %reshape.898), kind=kCustom, calls=%fused_computation.1.clone | custom fusion | bytes 2626560 | tf_op jit(solution)/shard_map/jit(take_along_axis)/gather | solution.py:144
  613.9 0.3 select_select_fusion.1
  614.1 0.4 bitcast_convert_fusion
  614.5 96.5 %scatter_fusion = f32[2,1024,1024]{2,1,0:T(8,128)} fusion(f32[2,1024,1024]{2,1,0:T(8,128)} %convert_element_type.47, s32[640]{0:T(1024)S(1)} %reshape.881, f32[640,1024]{1,0:T(8,128)S(1)} %bitcast_convert_fusion), kind=kCustom, calls=%fused_computation.6 | custom fusion | flops 655360 | bytes 7869440 | tf_op jit(solution)/shard_map/scatter-add | solution.py:154
  (52 shorter events, 1.9 us)
Async XLA Ops:
  33.2 35.2 %all-to-all-start = ((bf16[2,16,20,1024]{3,0,2,1:T(2,128)(2,1)}), bf16[2,16,20,1024]{3,0,2,1:T(2,128)(2,1)S(1)}, u32[]{:S(2)}, u32[]{:S(2)}) async-start(bf16[2,16,20,1024]{3,0,2,1:T(2,128)(2,1)} %bitcast.9), calls=%async_computation | async-start | bytes 2621440 | tf_op jit(solution)/shard_map/all_to_all | solution.py:42
  51.6 55.6 %all-gather.8.cloned.1.call-start = ((), (), s32[]{:S(2)}) async-start(), calls=%async_computation.3 | async-start | bytes 4718592 | tf_op jit(solution)/shard_map/all_gather | solution.py:53
  71.5 38.9 %copy-start.2 = (f32[8192]{0:T(1024)S(1)}, f32[8192]{0:T(1024)}, u32[]{:S(2)}) copy-start(f32[8192]{0:T(1024)} %param.17) | copy-start | bytes 98308
  72.5 79.9 %all-gather.14.cloned.1.call-start = ((), (), s32[]{:S(2)}) async-start(), calls=%async_computation.6 | async-start | bytes 2228224 | tf_op jit(solution)/shard_map/all_gather | solution.py:69
  73.2 125.4 %all-gather.10.cloned.1.call-start = ((), (), s32[]{:S(2)}) async-start(), calls=%async_computation.4 | async-start | bytes 2228224 | tf_op jit(solution)/shard_map/all_gather | solution.py:74
  74.0 237.5 %all-gather.18.cloned.1.call-start = ((), (), s32[]{:S(2)}) async-start(), calls=%async_computation.8 | async-start | bytes 17825792 | tf_op jit(solution)/shard_map/all_gather | solution.py:64
  74.5 280.6 %all-gather.16.cloned.1.call-start = ((), (), s32[]{:S(2)}) async-start(), calls=%async_computation.7 | async-start | bytes 1114112 | tf_op jit(solution)/shard_map/all_gather | solution.py:84
  107.2 3.4 copy-start.1
  157.1 47.3 %copy-start.4 = (s32[2,16,16]{2,1,0:T(8,128)S(1)}, s32[2,16,16]{2,1,0:T(8,128)}, u32[]{:S(2)}) copy-start(s32[2,16,16]{2,1,0:T(8,128)} %param.15) | copy-start | bytes 6148
  157.1 242.5 %all-gather.12.cloned.1.call-start = ((), (), s32[]{:S(2)}) async-start(), calls=%async_computation.5 | async-start | bytes 1114112 | tf_op jit(solution)/shard_map/all_gather | solution.py:85
  203.5 317.3 %all-gather.20.cloned.1.call-start = ((), (), s32[]{:S(2)}) async-start(), calls=%async_computation.9 | async-start | bytes 17825792 | tf_op jit(solution)/shard_map/all_gather | solution.py:120
  204.3 368.1 %reduce-scatter.2.cloned.1.call-start = ((), (), s32[]{:S(2)}) async-start(), calls=%async_computation.10 | async-start | bytes 4718592 | tf_op jit(solution)/shard_map/reduce_scatter | solution.py:123
  359.0 5.7 copy-start
  533.0 0.7 copy-start.3
  533.0 0.8 copy-start.5
  584.1 21.9 %all-to-all-start.1 = ((bf16[2,16,20,1024]{3,0,2,1:T(2,128)(2,1)}), bf16[2,16,20,1024]{3,0,2,1:T(2,128)(2,1)S(1)}, u32[]{:S(2)}, u32[]{:S(2)}) async-start(bf16[2,16,20,1024]{3,0,2,1:T(2,128)(2,1)} %copy.57), calls=%async_computation.2 | async-start | bytes 2621440 | tf_op jit(solution)/shard_map/all_to_all | solution.py:138
Sparse Core Ops, SparseCore 0:
  72.6 34.5 all-gather.7
  109.3 42.9 all-gather.13
  154.5 44.1 all-gather.9
  200.7 110.7 all-gather.17
  313.4 41.7 all-gather.15
  357.2 42.3 all-gather.11
  401.7 119.0 all-gather.19
  533.2 39.1 reduce-scatter.1
where the time goes:
time: 731 us; the launch traced here: 718 us
  waiting for transfers between devices  450 us (62%)
  other arithmetic  121 us (17%)
  local copies, waits for them, and re-layouts  55.5 us (8%)
  matrix products  50.8 us (7%)
  starting transfers between devices  26.7 us (4%)
  between operations  14.1 us (2%)
    all_gather x1, waiting for transfers between devices, shards(): lax.all_gather(w_out, 'fsdp', axis=1, tiled=True)  111 us
    all_gather x1, waiting for transfers between devices, shards(): lax.all_gather(w_query, 'fsdp', axis=0, tiled=True)  105 us
    scatter-add x1, other arithmetic, shards(): result.at[seq_ids, keep_index].add(landed.astype(jnp.float32), mode='drop')  96.5 us
    all_gather x1, waiting for transfers between devices, shards(): lax.all_gather(w_value, 'fsdp', axis=0, tiled=True)  41.5 us
    all_gather x1, waiting for transfers between devices, shards(): lax.all_gather(w_key, 'fsdp', axis=0, tiled=True)  38.3 us
    reduce_scatter x1, waiting for transfers between devices, shards(): lax.psum_scatter(partial_value.reshape(seq_count, own_rows, full_width).a...  35 us
    all_gather x1, waiting for transfers between devices, shards(): full_rows = lax.all_gather(narrow_rows, 'seq', axis=2, tiled=True)  32.1 us
    all_gather x1, waiting for transfers between devices, shards(): lax.all_gather(key_rows, 'fsdp', axis=1, tiled=True)  32.1 us
  transfers between devices with their start and end apart: 10, of which 10 were waited for; matrix products, arithmetic and copies ran while one was open for 9% of the time, Pallas kernels for 0%

commit v1 on v0

v1 whole, which is shorter than its diff:
```python
import math

import jax
import jax.numpy as jnp
from jax import lax
from jax.sharding import PartitionSpec as P

HD = 128
BLK = 128


epsilon = 1e-05


def onehot(index, size):
    return (index[..., None] == jnp.arange(size, dtype=jnp.int32)).astype(jnp.bfloat16)


def select_rows(index, rows):
    picked = jnp.einsum(
        "skp,spc->skc", onehot(index, rows.shape[1]), rows, preferred_element_type=jnp.float32
    )
    return picked.astype(rows.dtype)


def small_take(table, index):
    hits = index[..., None] == jnp.arange(table.shape[1], dtype=jnp.int32)
    return jnp.sum(jnp.where(hits, table[:, None, :], 0), axis=-1)


def gather_all(x, axis_name, count):
    copies = jnp.broadcast_to(x[None], (count,) + x.shape)
    return lax.all_to_all(copies, axis_name, split_axis=0, concat_axis=0, tiled=True)


def shards(
    tokens, keep_index, keep_count, block_mask, router, norm_gain, w_query, w_key, w_value, w_out
):
    fsdp_size = lax.axis_size("fsdp")
    seq_size = lax.axis_size("seq")
    owner_idx = lax.axis_index("fsdp")
    seq_count, tok_dev, part_width = tokens.shape
    kept_most = keep_index.shape[1]
    slot_count = kept_most // fsdp_size
    own_rows = tok_dev // 8
    block_count = block_mask.shape[1]

    in_rows, q_cols = w_query.shape
    kv_cols = w_key.shape[1]
    qkv_local = jnp.concatenate([w_query, w_key, w_value], axis=1)
    packed = jnp.concatenate([qkv_local.reshape(-1), w_out.reshape(-1)])
    gathered = lax.all_gather(packed, "fsdp", axis=0, tiled=False)
    qkv_size = qkv_local.size
    w_qkv = gathered[:, :qkv_size].reshape(fsdp_size * in_rows, q_cols + 2 * kv_cols)
    w_out_blocks = gathered[:, qkv_size:].reshape((fsdp_size,) + w_out.shape)

    starts = jnp.cumsum(keep_count, axis=1) - keep_count
    range_ends = starts + keep_count
    my_start = lax.dynamic_index_in_dim(starts, owner_idx, 1, keepdims=False)
    my_count = lax.dynamic_index_in_dim(keep_count, owner_idx, 1, keepdims=False)

    owner_ids = jnp.arange(fsdp_size, dtype=jnp.int32)[None, :, None]
    slot_ids = jnp.arange(slot_count, dtype=jnp.int32)[None, None, :]
    first_pick = jnp.mod(owner_ids - my_start[:, None, None], fsdp_size)
    pick_index = (first_pick + slot_ids * fsdp_size).reshape(seq_count, -1)
    usable = pick_index < my_count[:, None]
    src_pos = small_take(keep_index, jnp.minimum(pick_index, kept_most - 1))
    src_pos = jnp.where(usable, src_pos, -1)
    send_rows = select_rows(src_pos, tokens).reshape(seq_count, fsdp_size, slot_count, part_width)
    received = lax.all_to_all(send_rows, "fsdp", split_axis=1, concat_axis=1, tiled=True)

    kept_rank = jnp.arange(own_rows, dtype=jnp.int32) * fsdp_size + owner_idx
    source = jnp.sum((range_ends[:, None, :] <= kept_rank[None, :, None]).astype(jnp.int32), axis=2)
    source_start = small_take(starts, source)
    slot_of = (kept_rank[None, :] - source_start) // fsdp_size
    flat_index = source * slot_count + slot_of
    narrow_rows = select_rows(
        flat_index, received.reshape(seq_count, fsdp_size * slot_count, part_width)
    )
    row_parts = gather_all(narrow_rows, "seq", seq_size)
    full_rows = jnp.transpose(row_parts, (1, 2, 0, 3)).reshape(
        seq_count, own_rows, seq_size * part_width
    )
    full_width = full_rows.shape[2]
    row_total = seq_count * own_rows
    flat_rows = full_rows.reshape(row_total, full_width)
    router_logit = jnp.dot(flat_rows, router, preferred_element_type=jnp.float32)
    gate_value = jax.nn.sigmoid(router_logit)
    wide = flat_rows.astype(jnp.float32)
    mean_square = jnp.mean(wide * wide, axis=1, keepdims=True)
    normed = (wide * lax.rsqrt(mean_square + epsilon) * norm_gain).astype(jnp.bfloat16)
    qkv_sum = jnp.dot(normed, w_qkv, preferred_element_type=jnp.float32).astype(jnp.bfloat16)
    local_kv = kv_cols // HD
    local_heads = q_cols // HD
    group_size = local_heads // local_kv
    queries = qkv_sum[:, :q_cols].reshape(seq_count, own_rows, local_kv, group_size, HD)
    kv_rows = qkv_sum[:, q_cols:].reshape(seq_count, own_rows, 2 * kv_cols)
    kv_parts = gather_all(kv_rows, "fsdp", fsdp_size)
    keep_total = fsdp_size * own_rows
    all_kv = jnp.transpose(kv_parts, (1, 0, 2, 3)).reshape(seq_count, keep_total, 2 * kv_cols)
    key_position = jnp.arange(keep_total, dtype=jnp.int32)
    key_rank = key_position % own_rows * fsdp_size + key_position // own_rows
    block_ids = jnp.arange(block_count, dtype=jnp.int32)
    query_onehot = (kept_rank[:, None] // BLK == block_ids[None, :]).astype(jnp.float32)
    key_onehot = (key_rank[:, None] // BLK == block_ids[None, :]).astype(jnp.float32)
    block_open = jnp.einsum(
        "qa,sab,tb->sqt", query_onehot, block_mask.astype(jnp.float32), key_onehot
    )
    allowed = (block_open > 0.5) & (key_rank[None, None, :] <= kept_rank[None, :, None])
    open_mask = allowed[:, None, None, :, :]
    key_heads = all_kv[:, :, :kv_cols].reshape(seq_count, keep_total, local_kv, HD)
    value_heads = all_kv[:, :, kv_cols:].reshape(seq_count, keep_total, local_kv, HD)
    scores = jnp.einsum(
        "sqkgd,stkd->skgqt", queries, key_heads, preferred_element_type=jnp.float32
    ) * (1.0 / math.sqrt(HD))
    scores = jnp.where(open_mask, scores, jnp.float32(-1e30))
    row_max = jnp.max(scores, axis=4, keepdims=True)
    weights = jnp.where(open_mask, jnp.exp(scores - row_max), jnp.float32(0.0))
    totals = jnp.sum(weights, axis=4, keepdims=True)
    mixed_values = jnp.einsum(
        "skgqt,stkd->sqkgd",
        weights.astype(jnp.bfloat16),
        value_heads,
        preferred_element_type=jnp.float32,
    )
    attended = (
        (mixed_values / jnp.transpose(totals, (0, 3, 1, 2, 4)))
        .astype(jnp.bfloat16)
        .reshape(row_total, local_heads * HD)
    )
    partial_value = jnp.einsum(
        "rk,fkc->rfc", attended, w_out_blocks, preferred_element_type=jnp.float32
    )
    summed = lax.psum_scatter(
        partial_value.reshape(seq_count, own_rows, full_width).astype(jnp.bfloat16),
        "seq",
        scatter_dimension=2,
        tiled=True,
    ).astype(jnp.float32)
    update = (gate_value.reshape(seq_count, own_rows, 1) * summed).astype(jnp.bfloat16)

    first_back = jnp.mod(owner_idx - starts, fsdp_size)[:, :, None]
    back_pick = first_back + slot_ids * fsdp_size
    back_usable = (back_pick < keep_count[:, :, None]).reshape(seq_count, -1)
    back_slot = ((starts[:, :, None] + back_pick) // fsdp_size).reshape(seq_count, -1)
    back_slot = jnp.where(back_usable, back_slot, -1)
    back_rows = select_rows(back_slot, update).reshape(
        seq_count, fsdp_size, slot_count, part_width
    )
    returned = lax.all_to_all(back_rows, "fsdp", split_axis=1, concat_axis=1, tiled=True)
    kept_pos = jnp.arange(kept_most, dtype=jnp.int32)
    their_owner = jnp.mod(my_start[:, None] + kept_pos[None, :], fsdp_size)
    flat_back = their_owner * slot_count + kept_pos[None, :] // fsdp_size
    flat_back = jnp.where(kept_pos[None, :] < my_count[:, None], flat_back, -1)
    landed = select_rows(
        flat_back, returned.reshape(seq_count, fsdp_size * slot_count, part_width)
    )
    valid_pos = jnp.where(kept_pos[None, :] < my_count[:, None], keep_index, -1)
    dense_update = jnp.einsum(
        "skp,skc->spc", onehot(valid_pos, tok_dev), landed, preferred_element_type=jnp.float32
    )
    return tokens.astype(jnp.float32) + dense_update


def solution(mesh):
    placed = (
        P(None, "fsdp", "seq"),
        P(None, "fsdp"),
        P(),
        P(),
        P(),
        P(),
        P("fsdp", "seq"),
        P("fsdp", "seq"),
        P("fsdp", "seq"),
        P("seq", "fsdp"),
    )
    return jax.shard_map(
        shards, mesh=mesh, in_specs=placed, out_specs=P(None, "fsdp", "seq"), check_vma=False
    )
```

time: 731 us -> 510 us (0.70)
  the two profiles are of different devices: /device:TPU:26 before, /device:TPU:0 now
where the time goes in v1:
time: 510 us; the launch traced here: 502 us
  waiting for transfers between devices  224 us (44%)
  local copies, waits for them, and re-layouts  157 us (31%)
  matrix products  45.8 us (9%)
  blocking collectives  23.8 us (5%)
  other arithmetic  18.9 us (4%)
  starting transfers between devices  18.2 us (4%)
  between operations  14.2 us (3%)
    all_gather x1, waiting for transfers between devices, shards(): gathered = lax.all_gather(packed, 'fsdp', axis=0, tiled=False)  111 us
    all_to_all x2, waiting for transfers between devices, gather_all(): lax.all_to_all(copies, axis_name, split_axis=0, concat_axis=0, tiled=True)  49.7 us
    all_gather x1, local copies, waits for them, and re-layouts, shards(): gathered = lax.all_gather(packed, 'fsdp', axis=0, tiled=False)  41.8 us
    all_to_all x1, waiting for transfers between devices, shards(): lax.all_to_all(send_rows, 'fsdp', split_axis=1, concat_axis=1, tiled=True)  34.6 us
    reduce_scatter x1, waiting for transfers between devices, shards(): lax.psum_scatter(partial_value.reshape(seq_count, own_rows, full_width).a...  29.2 us
    unnamed x17, local copies, waits for them, and re-layouts  26 us
    reshape x1, local copies, waits for them, and re-layouts, shards(): gathered[:, :qkv_size].reshape(fsdp_size * in_rows, q_cols + 2 * kv_cols)  25.3 us
    all_to_all x1, blocking collectives, shards(): lax.all_to_all(back_rows, 'fsdp', split_axis=1, concat_axis=1, tiled=True)  23.8 us
  transfers between devices with their start and end apart: 5, of which 4 were waited for; matrix products, arithmetic and copies ran while one was open for 15% of the time, Pallas kernels for 0%

profile of v1, /device:TPU:0, one launch (start us, length us, event | category | flops | bytes accessed | tf_op | source)
XLA Modules:
  0.0 502.1 jit_solution(8536541599219903088)
XLA Ops:
  6.5 2.6 copy.69
  9.1 1.5 pad_maximum_fusion.1
  10.6 1.5 reshape.557
  12.1 5.2 %pad_maximum_fusion = bf16[1179648]{0:T(1024)(128)(2,1)} fusion(bf16[524288]{0:T(1024)(128)(2,1)} %bitcast.111, bf16[655360]{0:T(1024)(128)(2,1)S(1)} %reshape.557), kind=kLoop, calls=%fused_computation.20 | loop fusion | flops 4718592 | bytes 4718592 | tf_op jit(solution)/shard_map/concatenate | solution.py:51
  17.4 0.2 reduce_window_sum.11
  17.6 0.1 add.247
  17.7 0.1 add.250
  17.8 0.1 add.251
  17.9 0.2 dynamic-slice_reduce_fusion
  18.1 0.1 and_select_fusion.3
  18.2 0.1 add.257
  18.2 0.1 add.258
  18.3 0.1 add.244
  18.4 0.1 add.245
  18.5 0.1 lt.92
  18.6 0.1 lt.93
  18.7 0.3 select_reduce_fusion
  19.0 0.1 compare_select_fusion.3
  19.1 3.8 fusion.12
  22.8 2.4 copy.47
  25.3 7.1 %all-to-all-start = ((bf16[2,16,20,1024]{3,0,2,1:T(2,128)(2,1)}), bf16[2,16,20,1024]{3,0,2,1:T(2,128)(2,1)S(1)}, u32[]{:S(2)}, u32[]{:S(2)}) async-start(bf16[2,16,20,1024]{3,0,2,1:T(2,128)(2,1)} %bitcast), calls=%async_computation | async-start | bytes 2621440 | tf_op jit(solution)/shard_map/all_to_all | solution.py:70
  32.4 0.1 convert_reduce_fusion
  32.5 0.1 select_reduce_fusion.1
  32.6 34.6 %all-to-all-done = bf16[2,16,20,1024]{3,0,2,1:T(2,128)(2,1)S(1)} async-done(((bf16[2,16,20,1024]{3,0,2,1:T(2,128)(2,1)}), bf16[2,16,20,1024]{3,0,2,1:T(2,128)(2,1)S(1)}, u32[]{:S(2)}, u32[]{:S(2)}) %all-to-all-start) | async-done | bytes 1310752 | tf_op jit(solution)/shard_map/all_to_all | solution.py:70
  67.3 0.6 fusion.21
  67.9 2.6 broadcast_in_dim.62
  70.4 5.7 %all-to-all-start.1 = ((bf16[8,2,128,1024]{3,2,1,0:T(8,128)(2,1)}), bf16[8,2,128,1024]{3,2,1,0:T(8,128)(2,1)}, u32[]{:S(2)}, u32[]{:S(2)}) async-start(bf16[8,2,128,1024]{3,2,1,0:T(8,128)(2,1)} %broadcast_in_dim.62), calls=%async_computation.1 | async-start | bytes 8388608 | tf_op jit(solution)/shard_map/all_to_all | solution.py:33
  76.2 49.6 %all-to-all-done.1 = bf16[8,2,128,1024]{3,2,1,0:T(8,128)(2,1)} async-done(((bf16[8,2,128,1024]{3,2,1,0:T(8,128)(2,1)}), bf16[8,2,128,1024]{3,2,1,0:T(8,128)(2,1)}, u32[]{:S(2)}, u32[]{:S(2)}) %all-to-all-start.1) | async-done | bytes 4194336 | tf_op jit(solution)/shard_map/all_to_all | solution.py:33
  125.8 3.3 fusion.3
  129.1 3.8 fusion.5
  132.9 2.3 copy.50
  135.2 6.3 %copy.68 = bf16[32,8,8,1024]{3,1,2,0:T(8,128)(2,1)} copy(bf16[32,8,8,1024]{3,2,1,0:T(8,128)(2,1)S(1)} %bitcast.106) | data formatting | bytes 8388608
  141.6 110.5 %all-gather.3.cloned.1.call-done = bf16[18874368]{0:T(1024)(128)(2,1)} async-done(((bf16[1179648]{0:T(1024)(128)(2,1)}), bf16[18874368]{0:T(1024)(128)(2,1)}) %all-gather.3.cloned.1.call-update) | async-done | bytes 37748752 | tf_op jit(solution)/shard_map/all_gather | solution.py:52
  252.1 41.8 %reshape.566 = bf16[16,1179648]{1,0:T(8,128)(2,1)} reshape(bf16[18874368]{0:T(1024)(128)(2,1)} %all-gather.3.cloned.1.call-done) | data formatting | bytes 75497472 | tf_op jit(solution)/shard_map/all_gather | solution.py:52
  293.9 17.1 %slice.24 = bf16[16,655360]{1,0:T(8,128)(2,1)} slice(bf16[16,1179648]{1,0:T(8,128)(2,1)} %reshape.566), slice={[0:16], [0:655360]} | slice | bytes 41943040 | tf_op jit(solution)/shard_map/slice | solution.py:54
  311.0 25.3 %reshape.559 = bf16[8192,1280]{1,0:T(8,128)(2,1)} reshape(bf16[16,655360]{1,0:T(8,128)(2,1)} %slice.24) | data formatting | bytes 41943040 | tf_op jit(solution)/shard_map/reshape | solution.py:54
  336.2 13.4 %convolution_convert_fusion.1 = bf16[256,1280]{1,0:T(8,128)(2,1)S(1)} fusion(bf16[256,8192]{1,0:T(8,128)(2,1)} %bitcast.110, bf16[8192,1280]{1,0:T(8,128)(2,1)} %reshape.559), kind=kOutput, calls=%fused_computation.18 | convolution fusion | flops 5369036800 | bytes 25821184 | tf_op jit(solution)/shard_map/dot_general | solution.py:92
  349.7 1.6 broadcast_in_dim.64
  351.2 5.3 %all-to-all-start.2 = ((bf16[16,2,128,256]{3,2,1,0:T(8,128)(2,1)}), bf16[16,2,128,256]{3,2,1,0:T(8,128)(2,1)S(1)}, u32[]{:S(2)}, u32[]{:S(2)}) async-start(bf16[16,2,128,256]{3,2,1,0:T(8,128)(2,1)} %broadcast_in_dim.64), calls=%async_computation.2 | async-start | bytes 4194304 | tf_op jit(solution)/shard_map/all_to_all | solution.py:33
  356.5 0.0 reduce-scatter.2.cloned.1.call-start
  356.6 0.1 copy.52
  356.7 0.1 fusion.48
  356.8 0.2 broadcast_compare_fusion
  357.0 1.4 fusion.11
  358.4 2.1 copy.53
  360.5 5.8 %slice-done = bf16[16,524288]{1,0:T(8,128)(2,1)S(1)} async-done(((bf16[16,1179648]{1,0:T(8,128)(2,1)}), bf16[16,524288]{1,0:T(8,128)(2,1)S(1)}, s32[]{:S(2)}) %slice-start) | async-done | bytes 16777240 | tf_op jit(solution)/shard_map/slice | solution.py:55
  366.3 11.8 %copy.71 = bf16[2,8,1024,512]{3,2,1,0:T(8,128)(2,1)} copy(bf16[2,8,1024,512]{3,1,2,0:T(8,128)(2,1)S(1)} %bitcast.102) | data formatting | bytes 33554432
  378.2 21.7 %copy.57 = bf16[16,512,1024]{2,1,0:T(8,128)(2,1)} copy(bf16[16,512,1024]{1,2,0:T(8,128)(2,1)} %bitcast.103) | data formatting | bytes 33554432 | tf_op jit(solution)/shard_map/rk,fkc->rfc/dot_general | solution.py:131
  399.9 0.1 slice_bitcast_fusion.6
  399.9 0.1 copy.70
  400.1 0.2 copy.51
  400.3 2.7 fusion
  403.0 4.1 fusion.1
  407.1 4.2 divide_convert_fusion
  411.3 9.7 %convolution_convert_fusion = bf16[2,128,8192]{2,1,0:T(8,128)(2,1)} fusion(bf16[2,128,1024]{1,2,0:T(8,128)(2,1)S(1)} %bitcast.123, bf16[8192,1024,1]{1,0,2:T(8,128)(2,1)} %bitcast.104), kind=kOutput, calls=%fused_computation.7 | convolution fusion | flops 4297064448 | bytes 21495808 | tf_op jit(solution)/shard_map/rk,fkc->rfc/dot_general | solution.py:131
  421.1 0.7 copy-done.1
  421.8 4.5 copy.49
  426.3 4.3 copy.67
  430.6 1.2 fusion.65
  431.8 29.2 %reduce-scatter.2.cloned.1.call-done = bf16[2,128,1024]{2,1,0:T(8,128)(2,1)} async-done(((bf16[2,128,8192]{2,1,0:T(8,128)(2,1)}), bf16[2,128,1024]{2,1,0:T(8,128)(2,1)}) %reduce-scatter.2.cloned.1.call-update) | async-done | bytes 524304 | tf_op jit(solution)/shard_map/reduce_scatter | solution.py:134
  461.0 1.6 convolution_convert_fusion.3
  462.6 1.3 copy.59
  464.0 23.8 %all_to_all.20 = bf16[2,16,20,1024]{3,0,2,1:T(2,128)(2,1)S(1)} all-to-all(bf16[2,16,20,1024]{3,0,2,1:T(2,128)(2,1)S(1)} %bitcast.109), channel_id=1, replica_groups=mesh['seq'=8,'fsdp'=16] {'fsdp'}, dimensions={1} | all-to-all | bytes 2621440 | tf_op jit(solution)/shard_map/all_to_all | solution.py:150
  487.8 7.0 %convert_add_fusion = f32[2,1024,1024]{2,1,0:T(8,128)} fusion(bf16[2,1024,1024]{2,1,0:T(8,128)(2,1)} %param.10, s32[2,320]{1,0:T(2,128)S(1)} %get-tuple-element.10, bf16[2,320,1024]{2,0,1:T(2,128)(2,1)S(1)} %bitcast.115, s32[2,320]{1,0:T(2,128)S(1)} %get-tuple-element.9), kind=kOutput, calls=%fused_computation.12 | convolution fusion | flops 1767317504 | bytes 13898752 | tf_op jit(solution)/shard_map/skp,skc->spc/dot_general | solution.py:159
  (30 shorter events, 0.2 us)
Async XLA Ops:
  6.5 245.6 %all-gather.3.cloned.1.call-start = ((), (), s32[]{:S(2)}) async-start(), calls=%async_computation.6 | async-start | bytes 40108032 | tf_op jit(solution)/shard_map/all_gather | solution.py:52
  12.1 5.3 %copy-start.3 = (s32[2,16]{1,0:T(2,128)S(1)}, s32[2,16]{1,0:T(2,128)}, u32[]{:S(2)}) copy-start(s32[2,16]{1,0:T(2,128)} %param.12) | copy-start | bytes 388
  12.1 6.6 %copy-start.4 = (s32[2,320]{1,0:T(2,128)S(1)}, s32[2,320]{1,0:T(2,128)}, u32[]{:S(2)}) copy-start(s32[2,320]{1,0:T(2,128)} %param.11) | copy-start | bytes 7684
  25.3 42.0 %all-to-all-start = ((bf16[2,16,20,1024]{3,0,2,1:T(2,128)(2,1)}), bf16[2,16,20,1024]{3,0,2,1:T(2,128)(2,1)S(1)}, u32[]{:S(2)}, u32[]{:S(2)}) async-start(bf16[2,16,20,1024]{3,0,2,1:T(2,128)(2,1)} %bitcast), calls=%async_computation | async-start | bytes 2621440 | tf_op jit(solution)/shard_map/all_to_all | solution.py:70
  70.4 5.8 %copy-start = (f32[8192]{0:T(1024)S(1)}, f32[8192]{0:T(1024)}, u32[]{:S(2)}) copy-start(f32[8192]{0:T(1024)} %param.15) | copy-start | bytes 98308
  70.4 55.4 %all-to-all-start.1 = ((bf16[8,2,128,1024]{3,2,1,0:T(8,128)(2,1)}), bf16[8,2,128,1024]{3,2,1,0:T(8,128)(2,1)}, u32[]{:S(2)}, u32[]{:S(2)}) async-start(bf16[8,2,128,1024]{3,2,1,0:T(8,128)(2,1)} %broadcast_in_dim.62), calls=%async_computation.1 | async-start | bytes 8388608 | tf_op jit(solution)/shard_map/all_to_all | solution.py:33
  349.6 6.9 %copy-start.2 = (s32[2,16,16]{2,1,0:T(8,128)S(1)}, s32[2,16,16]{2,1,0:T(8,128)}, u32[]{:S(2)}) copy-start(s32[2,16,16]{2,1,0:T(8,128)} %param.13) | copy-start | bytes 6148
  351.2 48.8 %all-to-all-start.2 = ((bf16[16,2,128,256]{3,2,1,0:T(8,128)(2,1)}), bf16[16,2,128,256]{3,2,1,0:T(8,128)(2,1)S(1)}, u32[]{:S(2)}, u32[]{:S(2)}) async-start(bf16[16,2,128,256]{3,2,1,0:T(8,128)(2,1)} %broadcast_in_dim.64), calls=%async_computation.2 | async-start | bytes 4194304 | tf_op jit(solution)/shard_map/all_to_all | solution.py:33
  356.5 104.5 %reduce-scatter.2.cloned.1.call-start = ((), (), s32[]{:S(2)}) async-start(), calls=%async_computation.5 | async-start | bytes 4718592 | tf_op jit(solution)/shard_map/reduce_scatter | solution.py:134
  360.5 5.8 %slice-start = ((bf16[16,1179648]{1,0:T(8,128)(2,1)}), bf16[16,524288]{1,0:T(8,128)(2,1)S(1)}, s32[]{:S(2)}) async-start(bf16[16,1179648]{1,0:T(8,128)(2,1)} %reshape.566), calls=%async_computation.7 | async-start | bytes 33554432 | tf_op jit(solution)/shard_map/slice | solution.py:55
  421.1 0.7 copy-start.1
Sparse Core Ops, SparseCore 0:
  17.5 234.5 all-gather.2
  421.2 39.7 reduce-scatter.1

commit v2 on v1

--- a/solution.py
+++ b/solution.py
@@ -47,12 +47,11 @@
 
     in_rows, q_cols = w_query.shape
     kv_cols = w_key.shape[1]
-    qkv_local = jnp.concatenate([w_query, w_key, w_value], axis=1)
-    packed = jnp.concatenate([qkv_local.reshape(-1), w_out.reshape(-1)])
-    gathered = lax.all_gather(packed, "fsdp", axis=0, tiled=False)
-    qkv_size = qkv_local.size
-    w_qkv = gathered[:, :qkv_size].reshape(fsdp_size * in_rows, q_cols + 2 * kv_cols)
-    w_out_blocks = gathered[:, qkv_size:].reshape((fsdp_size,) + w_out.shape)
+    qkv_cols = q_cols + 2 * kv_cols
+    packed = jnp.concatenate([w_query, w_key, w_value, w_out.T], axis=1)
+    gathered = lax.all_gather(packed, "fsdp", axis=0, tiled=True)
+    w_qkv = gathered[:, :qkv_cols]
+    w_out_t = gathered[:, qkv_cols:]
 
     starts = jnp.cumsum(keep_count, axis=1) - keep_count
     range_ends = starts + keep_count
@@ -129,7 +128,7 @@
         .reshape(row_total, local_heads * HD)
     )
     partial_value = jnp.einsum(
-        "rk,fkc->rfc", attended, w_out_blocks, preferred_element_type=jnp.float32
+        "rk,nk->rn", attended, w_out_t, preferred_element_type=jnp.float32
     )
     summed = lax.psum_scatter(
         partial_value.reshape(seq_count, own_rows, full_width).astype(jnp.bfloat16),

time: 510 us -> 396 us (0.78); the launches traced: 502 us -> 396 us
  local copies, waits for them, and re-layouts: 157 us -> 19.9 us
  blocking collectives: 23.8 us -> 78.5 us
  waiting for transfers between devices: 224 us -> 213 us
  other arithmetic: 18.9 us -> 9.03 us
  starting transfers between devices: 18.2 us -> 12.4 us
    all_to_all x0 -> x1, blocking collectives: none -> 54.8 us  [gather_all(): lax.all_to_all(copies, axis_name, split_axis=0, concat_axis=0, tiled=True)]
    all_gather x1 -> x0, local copies, waits for them, and re-layouts: 41.8 us -> none  [shards(): gathered = lax.all_gather(packed, 'fsdp', axis=0, tiled=False)]
    reshape x2 -> x0, local copies, waits for them, and re-layouts: 26.7 us -> none  [the longest x1 25.3 us: shards(): gathered[:, :qkv_size].reshape(fsdp_size * in_rows, q_cols + 2 * kv_cols)]
    slice x3 -> x0, local copies, waits for them, and re-layouts: 22.9 us -> none  [the longest x1 17.1 us: shards(): gathered[:, :qkv_size].reshape(fsdp_size * in_rows, q_cols + 2 * kv_cols)]
    all_to_all x2 -> x1, waiting for transfers between devices: 49.7 us -> 27.3 us  [gather_all(): lax.all_to_all(copies, axis_name, split_axis=0, concat_axis=0, tiled=True)]
    dot_general x1 -> x0, local copies, waits for them, and re-layouts: 21.7 us -> none  [shards(): jnp.einsum('rk,fkc->rfc', attended, w_out_blocks, preferred_element_type=...]
    unnamed x17 -> x15, local copies, waits for them, and re-layouts: 26 us -> 8.73 us
    all_gather x1, waiting for transfers between devices: 111 us -> 119 us  [shards(): gathered = lax.all_gather(packed, 'fsdp', axis=0, tiled=True)]
  transfers between devices with their start and end apart: 5 -> 4, of which waited for: 4 -> 4; matrix products, arithmetic and copies ran while one was open for 15% -> 7% of each run, Pallas kernels for 0% -> 0%
where the time goes in v2:
time: 396 us
  waiting for transfers between devices  213 us (54%)
  blocking collectives  78.5 us (20%)
  matrix products  48.8 us (12%)
  local copies, waits for them, and re-layouts  19.9 us (5%)
  between operations  13.7 us (3%)
  starting transfers between devices  12.4 us (3%)
  other arithmetic  9.03 us (2%)
    all_gather x1, waiting for transfers between devices, shards(): gathered = lax.all_gather(packed, 'fsdp', axis=0, tiled=True)  119 us
    all_to_all x1, blocking collectives, gather_all(): lax.all_to_all(copies, axis_name, split_axis=0, concat_axis=0, tiled=True)  54.8 us
    all_to_all x1, waiting for transfers between devices, shards(): lax.all_to_all(send_rows, 'fsdp', split_axis=1, concat_axis=1, tiled=True)  34.6 us
    reduce_scatter x1, waiting for transfers between devices, shards(): lax.psum_scatter(partial_value.reshape(seq_count, own_rows, full_width).a...  32.2 us
    all_to_all x1, waiting for transfers between devices, gather_all(): lax.all_to_all(copies, axis_name, split_axis=0, concat_axis=0, tiled=True)  27.3 us
    all_to_all x1, blocking collectives, shards(): lax.all_to_all(back_rows, 'fsdp', split_axis=1, concat_axis=1, tiled=True)  23.7 us
    dot_general x1, matrix products, shards(): jnp.dot(normed, w_qkv, preferred_element_type=jnp.float32)  14 us
    dot_general x1, matrix products, shards(): jnp.einsum('rk,nk->rn', attended, w_out_t, preferred_element_type=jnp.flo...  9.93 us
  transfers between devices with their start and end apart: 4, of which 4 were waited for; matrix products, arithmetic and copies ran while one was open for 7% of the time, Pallas kernels for 0%

profile of v2, /device:TPU:0, one launch (start us, length us, event | category | flops | bytes accessed | tf_op | source)
XLA Modules:
  0.0 395.8 jit_solution(14154027433739378237)
XLA Ops:
  6.5 0.0 copy-start.2
  6.5 0.0 copy-start.3
  6.5 0.0 all-gather.2.cloned.1.call-start
  6.5 1.5 copy.44
  8.1 2.9 pad_maximum_fusion
  11.0 0.0 all-gather.2.cloned.1.call-update
  11.0 0.0 copy-done.2
  11.0 0.2 reduce_window_sum.11
  11.2 0.1 add.248
  11.3 0.1 add.251
  11.4 0.1 add.252
  11.5 0.2 dynamic-slice_reduce_fusion
  11.7 0.1 and_select_fusion.3
  11.8 0.1 add.258
  11.9 0.1 add.259
  12.0 0.1 add.245
  12.0 0.1 add.246
  12.1 0.1 lt.92
  12.2 0.1 lt.93
  12.3 0.0 copy-done.3
  12.3 0.3 select_reduce_fusion
  12.6 0.1 compare_select_fusion.3
  12.7 3.8 fusion.18
  16.5 2.4 copy.41
  18.9 7.1 %all-to-all-start = ((bf16[2,16,20,1024]{3,0,2,1:T(2,128)(2,1)}), bf16[2,16,20,1024]{3,0,2,1:T(2,128)(2,1)S(1)}, u32[]{:S(2)}, u32[]{:S(2)}) async-start(bf16[2,16,20,1024]{3,0,2,1:T(2,128)(2,1)} %bitcast), calls=%async_computation | async-start | bytes 2621440 | tf_op jit(solution)/shard_map/all_to_all | solution.py:69
  26.0 0.1 convert_reduce_fusion
  26.1 0.1 select_reduce_fusion.1
  26.2 34.6 %all-to-all-done = bf16[2,16,20,1024]{3,0,2,1:T(2,128)(2,1)S(1)} async-done(((bf16[2,16,20,1024]{3,0,2,1:T(2,128)(2,1)}), bf16[2,16,20,1024]{3,0,2,1:T(2,128)(2,1)S(1)}, u32[]{:S(2)}, u32[]{:S(2)}) %all-to-all-start) | async-done | bytes 1310752 | tf_op jit(solution)/shard_map/all_to_all | solution.py:69
  60.9 0.6 fusion.27
  61.5 0.5 broadcast_in_dim.62
  62.0 54.8 %all_to_all.20 = bf16[8,2,128,1024]{3,2,1,0:T(8,128)(2,1)S(1)} all-to-all(bf16[8,2,128,1024]{3,2,1,0:T(8,128)(2,1)S(1)} %broadcast_in_dim.62), channel_id=1, replica_groups=mesh['seq'=8,'fsdp'=16] {'seq'}, dimensions={0} | all-to-all | bytes 8388608 | tf_op jit(solution)/shard_map/all_to_all | solution.py:33
  116.8 2.3 copy.43
  119.2 6.3 %copy.60 = bf16[32,8,8,1024]{3,1,2,0:T(8,128)(2,1)} copy(bf16[32,8,8,1024]{3,2,1,0:T(8,128)(2,1)S(1)} %bitcast.97) | data formatting | bytes 8388608
  125.5 0.0 copy-start.4
  125.5 0.9 multiply_reduce_fusion
  126.4 119.3 %all-gather.2.cloned.1.call-done = bf16[8192,2304]{1,0:T(8,128)(2,1)} async-done(((bf16[512,2304]{1,0:T(8,128)(2,1)}), bf16[8192,2304]{1,0:T(8,128)(2,1)}) %all-gather.2.cloned.1.call-update) | async-done | bytes 37748752 | tf_op jit(solution)/shard_map/all_gather | solution.py:52
  245.7 0.0 copy-done.4
  245.7 14.0 %fusion.14 = bf16[256,1280]{1,0:T(8,128)(2,1)S(1)} fusion(bf16[8192,2304]{1,0:T(8,128)(2,1)} %all-gather.2.cloned.1.call-done, bf16[256,8192]{1,0:T(8,128)(2,1)} %bitcast.95, f32[8192]{0:T(1024)S(1)} %copy-done.4, f32[256]{0:T(256)S(1)} %rsqrt_bitcast_fusion), kind=kOutput, calls=%fused_computation.21 | convolution fusion | flops 5377425408 | bytes 25854976 | tf_op jit(solution)/shard_map/dot_general | solution.py:91
  259.8 0.0 copy-start.1
  259.8 1.5 broadcast_in_dim.64
  261.3 5.3 %all-to-all-start.2 = ((bf16[16,2,128,256]{3,2,1,0:T(8,128)(2,1)}), bf16[16,2,128,256]{3,2,1,0:T(8,128)(2,1)S(1)}, u32[]{:S(2)}, u32[]{:S(2)}) async-start(bf16[16,2,128,256]{3,2,1,0:T(8,128)(2,1)} %broadcast_in_dim.64), calls=%async_computation.2 | async-start | bytes 4194304 | tf_op jit(solution)/shard_map/all_to_all | solution.py:33
  266.6 0.0 reduce-scatter.2.cloned.1.call-start
  266.7 0.0 copy-done.1
  266.7 0.1 copy.46
  266.8 0.1 fusion.54
  266.9 0.2 broadcast_compare_fusion
  267.2 1.4 fusion.17
  268.6 1.9 copy.47
  270.4 0.1 slice_bitcast_fusion.10
  270.5 0.1 copy.61
  270.6 27.3 %all-to-all-done.2 = bf16[16,2,128,256]{3,2,1,0:T(8,128)(2,1)S(1)} async-done(((bf16[16,2,128,256]{3,2,1,0:T(8,128)(2,1)}), bf16[16,2,128,256]{3,2,1,0:T(8,128)(2,1)S(1)}, u32[]{:S(2)}, u32[]{:S(2)}) %all-to-all-start.2) | async-done | bytes 2097184 | tf_op jit(solution)/shard_map/all_to_all | solution.py:33
  297.9 0.1 copy.45
  298.1 2.7 fusion.3
  300.8 4.0 %fusion.4 = f32[2,8,128]{2,1,0:T(8,128)S(1)} fusion(f32[2,2048,128,8]{2,1,3,0:T(8,128)S(1)} %get-tuple-element.12, f32[2,8,128]{2,1,0:T(8,128)S(1)} %get-tuple-element.11, pred[2,128,2048]{1,2,0:T(8,128)(4,1)S(1)} %copy.47), kind=kLoop, calls=%fused_computation.7 | loop fusion | flops 20969472 | bytes 17317888 | tf_op jit(solution)/shard_map/reduce_sum | solution.py:118
  304.9 4.2 %divide_convert_fusion = bf16[2,128,1,8,128]{1,4,3,0,2:T(8,128)(2,1)S(1)} fusion(f32[2,2048,128,8]{2,1,3,0:T(8,128)S(1)} %get-tuple-element.12, f32[2,8,128]{2,1,0:T(8,128)S(1)} %get-tuple-element.11, pred[2,128,2048]{1,2,0:T(8,128)(4,1)S(1)} %copy.47, bf16[2,2048,256]{2,1,0:T(8,128)(2,1)S(1)} %bitcast.102, f32[2,128,8]{1,2,0:T(8,128)S(1)} %bitcast.109), kind=kOutput, calls=%fused_computation.39 | convolution fusion | flops 1095237632 | bytes 18890752 | tf_op jit(solution)/shard_map/skgqt,stkd->sqkgd/dot_general | solution.py:119
  309.1 9.9 %fusion.6 = bf16[2,128,8192]{2,1,0:T(8,128)(2,1)} fusion(bf16[2,128,1024]{1,2,0:T(8,128)(2,1)S(1)} %bitcast.111, bf16[8192,2304]{1,0:T(8,128)(2,1)} %all-gather.2.cloned.1.call-done), kind=kOutput, calls=%fused_computation.9 | convolution fusion | flops 4297064448 | bytes 21495808 | tf_op jit(solution)/shard_map/rk,nk->rn/dot_general | solution.py:130
  319.0 0.0 reduce-scatter.2.cloned.1.call-update
  319.1 0.7 copy-done
  319.8 3.4 fusion.71
  323.2 32.2 %reduce-scatter.2.cloned.1.call-done = bf16[2,128,1024]{2,1,0:T(8,128)(2,1)} async-done(((bf16[2,128,8192]{2,1,0:T(8,128)(2,1)}), bf16[2,128,1024]{2,1,0:T(8,128)(2,1)}) %reduce-scatter.2.cloned.1.call-update) | async-done | bytes 524304 | tf_op jit(solution)/shard_map/reduce_scatter | solution.py:133
  355.3 1.6 convolution_convert_fusion.1
  357.0 1.3 copy.52
  358.3 23.7 %all_to_all.21 = bf16[2,16,20,1024]{3,0,2,1:T(2,128)(2,1)S(1)} all-to-all(bf16[2,16,20,1024]{3,0,2,1:T(2,128)(2,1)S(1)} %bitcast.99), channel_id=1, replica_groups=mesh['seq'=8,'fsdp'=16] {'fsdp'}, dimensions={1} | all-to-all | bytes 2621440 | tf_op jit(solution)/shard_map/all_to_all | solution.py:149
  382.0 7.0 %convert_add_fusion = f32[2,1024,1024]{2,1,0:T(8,128)} fusion(bf16[2,1024,1024]{2,1,0:T(8,128)(2,1)} %param.10, s32[2,320]{1,0:T(2,128)S(1)} %get-tuple-element.10, bf16[2,320,1024]{2,0,1:T(2,128)(2,1)S(1)} %bitcast.104, s32[2,320]{1,0:T(2,128)S(1)} %get-tuple-element.9), kind=kOutput, calls=%fused_computation.13 | convolution fusion | flops 1767317504 | bytes 13898752 | tf_op jit(solution)/shard_map/skp,skc->spc/dot_general | solution.py:158
  (16 shorter events, 0.1 us)
Async XLA Ops:
  6.5 4.5 %copy-start.2 = (s32[2,16]{1,0:T(2,128)S(1)}, s32[2,16]{1,0:T(2,128)}, u32[]{:S(2)}) copy-start(s32[2,16]{1,0:T(2,128)} %param.12) | copy-start | bytes 388
  6.5 5.8 %copy-start.3 = (s32[2,320]{1,0:T(2,128)S(1)}, s32[2,320]{1,0:T(2,128)}, u32[]{:S(2)}) copy-start(s32[2,320]{1,0:T(2,128)} %param.11) | copy-start | bytes 7684
  6.5 239.2 %all-gather.2.cloned.1.call-start = ((), (), s32[]{:S(2)}) async-start(), calls=%async_computation.5 | async-start | bytes 40108032 | tf_op jit(solution)/shard_map/all_gather | solution.py:52
  18.9 42.0 %all-to-all-start = ((bf16[2,16,20,1024]{3,0,2,1:T(2,128)(2,1)}), bf16[2,16,20,1024]{3,0,2,1:T(2,128)(2,1)S(1)}, u32[]{:S(2)}, u32[]{:S(2)}) async-start(bf16[2,16,20,1024]{3,0,2,1:T(2,128)(2,1)} %bitcast), calls=%async_computation | async-start | bytes 2621440 | tf_op jit(solution)/shard_map/all_to_all | solution.py:69
  125.5 120.2 %copy-start.4 = (f32[8192]{0:T(1024)S(1)}, f32[8192]{0:T(1024)}, u32[]{:S(2)}) copy-start(f32[8192]{0:T(1024)} %param.15) | copy-start | bytes 98308
  259.8 6.9 %copy-start.1 = (s32[2,16,16]{2,1,0:T(8,128)S(1)}, s32[2,16,16]{2,1,0:T(8,128)}, u32[]{:S(2)}) copy-start(s32[2,16,16]{2,1,0:T(8,128)} %param.13) | copy-start | bytes 6148
  261.3 36.6 %all-to-all-start.2 = ((bf16[16,2,128,256]{3,2,1,0:T(8,128)(2,1)}), bf16[16,2,128,256]{3,2,1,0:T(8,128)(2,1)S(1)}, u32[]{:S(2)}, u32[]{:S(2)}) async-start(bf16[16,2,128,256]{3,2,1,0:T(8,128)(2,1)} %broadcast_in_dim.64), calls=%async_computation.2 | async-start | bytes 4194304 | tf_op jit(solution)/shard_map/all_to_all | solution.py:33
  266.6 88.7 %reduce-scatter.2.cloned.1.call-start = ((), (), s32[]{:S(2)}) async-start(), calls=%async_computation.6 | async-start | bytes 4718592 | tf_op jit(solution)/shard_map/reduce_scatter | solution.py:133
  319.0 0.7 copy-start
Sparse Core Ops, SparseCore 0:
  11.1 234.5 all-gather.1
  319.2 36.1 reduce-scatter.1

commit v3 on v2

--- a/solution.py
+++ b/solution.py
@@ -48,10 +48,9 @@
     in_rows, q_cols = w_query.shape
     kv_cols = w_key.shape[1]
     qkv_cols = q_cols + 2 * kv_cols
-    packed = jnp.concatenate([w_query, w_key, w_value, w_out.T], axis=1)
-    gathered = lax.all_gather(packed, "fsdp", axis=0, tiled=True)
-    w_qkv = gathered[:, :qkv_cols]
-    w_out_t = gathered[:, qkv_cols:]
+    packed = jnp.concatenate([w_query, w_key, w_value], axis=1)
+    w_qkv = lax.all_gather(packed, "fsdp", axis=0, tiled=True)
+    w_out_t = lax.all_gather(w_out.T, "fsdp", axis=0, tiled=True)
 
     starts = jnp.cumsum(keep_count, axis=1) - keep_count
     range_ends = starts + keep_count

time: 396 us -> 382 us (0.965)
  waiting for transfers between devices: 213 us -> 201 us
    all_gather x1 -> x2, waiting for transfers between devices: 119 us -> 95 us  [the longest x1 62.5 us: shards(): w_out_t = lax.all_gather(w_out.T, 'fsdp', axis=0, tiled=True)]
    all_to_all x1, waiting for transfers between devices: 27.3 us -> 37 us  [gather_all(): lax.all_to_all(copies, axis_name, split_axis=0, concat_axis=0, tiled=True)]
    unnamed x15 -> x17, local copies, waits for them, and re-layouts: 8.73 us -> 8.54 us
  transfers between devices with their start and end apart: 4 -> 5, of which waited for: 4 -> 5; matrix products, arithmetic and copies ran while one was open for 7% -> 14% of each run, Pallas kernels for 0% -> 0%
where the time goes in v3:
time: 382 us
  waiting for transfers between devices  201 us (53%)
  blocking collectives  78.6 us (21%)
  matrix products  48.2 us (13%)
  local copies, waits for them, and re-layouts  19.8 us (5%)
  between operations  13.4 us (4%)
  starting transfers between devices  12.7 us (3%)
  other arithmetic  8.7 us (2%)
    all_gather x1, waiting for transfers between devices, shards(): w_out_t = lax.all_gather(w_out.T, 'fsdp', axis=0, tiled=True)  62.5 us
    all_to_all x1, blocking collectives, gather_all(): lax.all_to_all(copies, axis_name, split_axis=0, concat_axis=0, tiled=True)  54.8 us
    all_to_all x1, waiting for transfers between devices, gather_all(): lax.all_to_all(copies, axis_name, split_axis=0, concat_axis=0, tiled=True)  37 us
    all_to_all x1, waiting for transfers between devices, shards(): lax.all_to_all(send_rows, 'fsdp', split_axis=1, concat_axis=1, tiled=True)  34.7 us
    reduce_scatter x1, waiting for transfers between devices, shards(): lax.psum_scatter(partial_value.reshape(seq_count, own_rows, full_width).a...  33.9 us
    all_gather x1, waiting for transfers between devices, shards(): w_qkv = lax.all_gather(packed, 'fsdp', axis=0, tiled=True)  32.5 us
    all_to_all x1, blocking collectives, shards(): lax.all_to_all(back_rows, 'fsdp', split_axis=1, concat_axis=1, tiled=True)  23.8 us
    dot_general x1, matrix products, shards(): jnp.dot(normed, w_qkv, preferred_element_type=jnp.float32)  13.6 us
  transfers between devices with their start and end apart: 5, of which 5 were waited for; matrix products, arithmetic and copies ran while one was open for 14% of the time, Pallas kernels for 0%

profile of v3, /device:TPU:0, one launch (start us, length us, event | category | flops | bytes accessed | tf_op | source)
XLA Modules:
  0.0 381.9 jit_solution(11722335647908755391)
XLA Ops:
  6.5 0.0 all-gather.3.cloned.1.call-start
  6.5 2.6 pad_maximum_fusion
  9.2 0.0 all-gather.3.cloned.1.call-update
  9.2 0.0 all-gather.5.cloned.1.call-start
  9.2 0.0 copy-done
  9.2 1.3 copy.44
  10.6 0.0 all-gather.5.cloned.1.call-update
  10.6 0.0 copy-done.3
  10.6 0.2 reduce_window_sum.11
  10.8 0.2 dynamic-slice_reduce_fusion
  11.0 0.1 and_select_fusion.3
  11.1 0.1 add.258
  11.2 0.1 add.259
  11.3 0.1 add.248
  11.4 0.1 add.251
  11.4 0.1 add.252
  11.5 0.1 add.245
  11.6 0.1 add.246
  11.7 0.1 lt.92
  11.8 0.1 lt.93
  11.9 0.0 copy-done.4
  11.9 0.3 select_reduce_fusion
  12.2 0.1 compare_select_fusion.3
  12.3 3.8 fusion.18
  16.0 2.4 copy.35
  18.4 7.1 %all-to-all-start = ((bf16[2,16,20,1024]{3,0,2,1:T(2,128)(2,1)}), bf16[2,16,20,1024]{3,0,2,1:T(2,128)(2,1)S(1)}, u32[]{:S(2)}, u32[]{:S(2)}) async-start(bf16[2,16,20,1024]{3,0,2,1:T(2,128)(2,1)} %bitcast), calls=%async_computation | async-start | bytes 2621440 | tf_op jit(solution)/shard_map/all_to_all | solution.py:68
  25.6 0.1 convert_reduce_fusion
  25.7 0.1 select_reduce_fusion.1
  25.8 34.7 %all-to-all-done = bf16[2,16,20,1024]{3,0,2,1:T(2,128)(2,1)S(1)} async-done(((bf16[2,16,20,1024]{3,0,2,1:T(2,128)(2,1)}), bf16[2,16,20,1024]{3,0,2,1:T(2,128)(2,1)S(1)}, u32[]{:S(2)}, u32[]{:S(2)}) %all-to-all-start) | async-done | bytes 1310752 | tf_op jit(solution)/shard_map/all_to_all | solution.py:68
  60.5 0.6 fusion.27
  61.1 0.5 broadcast_in_dim.62
  61.7 54.8 %all_to_all.20 = bf16[8,2,128,1024]{3,2,1,0:T(8,128)(2,1)S(1)} all-to-all(bf16[8,2,128,1024]{3,2,1,0:T(8,128)(2,1)S(1)} %broadcast_in_dim.62), channel_id=1, replica_groups=mesh['seq'=8,'fsdp'=16] {'seq'}, dimensions={0} | all-to-all | bytes 8388608 | tf_op jit(solution)/shard_map/all_to_all | solution.py:33
  116.5 2.3 copy.37
  118.8 6.3 %copy.54 = bf16[32,8,8,1024]{3,1,2,0:T(8,128)(2,1)} copy(bf16[32,8,8,1024]{3,2,1,0:T(8,128)(2,1)S(1)} %bitcast.98) | data formatting | bytes 8388608
  125.2 0.9 multiply_reduce_fusion
  126.1 32.5 %all-gather.3.cloned.1.call-done = bf16[8192,1280]{1,0:T(8,128)(2,1)} async-done(((bf16[512,1280]{1,0:T(8,128)(2,1)}), bf16[8192,1280]{1,0:T(8,128)(2,1)}) %all-gather.3.cloned.1.call-update) | async-done | bytes 20971536 | tf_op jit(solution)/shard_map/all_gather | solution.py:52
  158.6 0.0 copy-done.5
  158.6 13.6 %fusion.16 = bf16[256,1280]{1,0:T(8,128)(2,1)S(1)} fusion(bf16[8192,1280]{1,0:T(8,128)(2,1)} %all-gather.3.cloned.1.call-done, bf16[256,8192]{1,0:T(8,128)(2,1)} %bitcast.96, f32[8192]{0:T(1024)S(1)} %copy-done.5, f32[256]{0:T(256)S(1)} %rsqrt_bitcast_fusion), kind=kOutput, calls=%fused_computation.20 | convolution fusion | flops 5377425408 | bytes 25854976 | tf_op jit(solution)/shard_map/dot_general | solution.py:90
  172.1 0.0 copy-start.2
  172.2 1.6 broadcast_in_dim.64
  173.8 5.3 %all-to-all-start.2 = ((bf16[16,2,128,256]{3,2,1,0:T(8,128)(2,1)}), bf16[16,2,128,256]{3,2,1,0:T(8,128)(2,1)S(1)}, u32[]{:S(2)}, u32[]{:S(2)}) async-start(bf16[16,2,128,256]{3,2,1,0:T(8,128)(2,1)} %broadcast_in_dim.64), calls=%async_computation.2 | async-start | bytes 4194304 | tf_op jit(solution)/shard_map/all_to_all | solution.py:33
  179.0 0.3 reduce-scatter.2.cloned.1.call-start
  179.3 0.1 copy.39
  179.5 0.1 fusion.54
  179.6 0.2 broadcast_compare_fusion
  179.8 1.4 fusion.17
  181.2 1.9 copy.40
  183.1 0.1 slice_bitcast_fusion.6
  183.1 0.1 copy.55
  183.3 37.0 %all-to-all-done.2 = bf16[16,2,128,256]{3,2,1,0:T(8,128)(2,1)S(1)} async-done(((bf16[16,2,128,256]{3,2,1,0:T(8,128)(2,1)}), bf16[16,2,128,256]{3,2,1,0:T(8,128)(2,1)S(1)}, u32[]{:S(2)}, u32[]{:S(2)}) %all-to-all-start.2) | async-done | bytes 2097184 | tf_op jit(solution)/shard_map/all_to_all | solution.py:33
  220.2 0.1 copy.38
  220.3 2.7 fusion.2
  223.1 4.0 %fusion.3 = f32[2,8,128]{2,1,0:T(8,128)S(1)} fusion(f32[2,2048,128,8]{2,1,3,0:T(8,128)S(1)} %get-tuple-element.12, f32[2,8,128]{2,1,0:T(8,128)S(1)} %get-tuple-element.11, pred[2,128,2048]{1,2,0:T(8,128)(4,1)S(1)} %copy.40), kind=kLoop, calls=%fused_computation.5 | loop fusion | flops 20969472 | bytes 17317888 | tf_op jit(solution)/shard_map/reduce_sum | solution.py:117
  227.1 4.2 %divide_convert_fusion = bf16[2,128,1,8,128]{1,4,3,0,2:T(8,128)(2,1)S(1)} fusion(f32[2,2048,128,8]{2,1,3,0:T(8,128)S(1)} %get-tuple-element.12, f32[2,8,128]{2,1,0:T(8,128)S(1)} %get-tuple-element.11, pred[2,128,2048]{1,2,0:T(8,128)(4,1)S(1)} %copy.40, bf16[2,2048,256]{2,1,0:T(8,128)(2,1)S(1)} %bitcast.103, f32[2,128,8]{1,2,0:T(8,128)S(1)} %bitcast.110), kind=kOutput, calls=%fused_computation.38 | convolution fusion | flops 1095237632 | bytes 18890752 | tf_op jit(solution)/shard_map/skgqt,stkd->sqkgd/dot_general | solution.py:118
  231.4 62.5 %all-gather.5.cloned.1.call-done = bf16[8192,1024]{1,0:T(8,128)(2,1)} async-done(((bf16[512,1024]{1,0:T(8,128)(2,1)}), bf16[8192,1024]{1,0:T(8,128)(2,1)}) %all-gather.5.cloned.1.call-update) | async-done | bytes 16777232 | tf_op jit(solution)/shard_map/all_gather | solution.py:53
  293.9 9.7 %fusion.5 = bf16[2,128,8192]{2,1,0:T(8,128)(2,1)} fusion(bf16[2,128,1024]{1,2,0:T(8,128)(2,1)S(1)} %bitcast.112, bf16[8192,1024]{1,0:T(8,128)(2,1)} %all-gather.5.cloned.1.call-done), kind=kOutput, calls=%fused_computation.7 | convolution fusion | flops 4297064448 | bytes 21495808 | tf_op jit(solution)/shard_map/rk,nk->rn/dot_general | solution.py:129
  303.6 0.0 reduce-scatter.2.cloned.1.call-update
  303.7 0.7 copy-done.1
  304.4 3.4 fusion.71
  307.8 33.9 %reduce-scatter.2.cloned.1.call-done = bf16[2,128,1024]{2,1,0:T(8,128)(2,1)} async-done(((bf16[2,128,8192]{2,1,0:T(8,128)(2,1)}), bf16[2,128,1024]{2,1,0:T(8,128)(2,1)}) %reduce-scatter.2.cloned.1.call-update) | async-done | bytes 524304 | tf_op jit(solution)/shard_map/reduce_scatter | solution.py:132
  341.6 1.6 convolution_convert_fusion.1
  343.3 1.3 copy.46
  344.6 23.8 %all_to_all.21 = bf16[2,16,20,1024]{3,0,2,1:T(2,128)(2,1)S(1)} all-to-all(bf16[2,16,20,1024]{3,0,2,1:T(2,128)(2,1)S(1)} %bitcast.100), channel_id=1, replica_groups=mesh['seq'=8,'fsdp'=16] {'fsdp'}, dimensions={1} | all-to-all | bytes 2621440 | tf_op jit(solution)/shard_map/all_to_all | solution.py:148
  368.4 7.0 %convert_add_fusion = f32[2,1024,1024]{2,1,0:T(8,128)} fusion(bf16[2,1024,1024]{2,1,0:T(8,128)(2,1)} %param.10, s32[2,320]{1,0:T(2,128)S(1)} %get-tuple-element.10, bf16[2,320,1024]{2,0,1:T(2,128)(2,1)S(1)} %bitcast.105, s32[2,320]{1,0:T(2,128)S(1)} %get-tuple-element.9), kind=kOutput, calls=%fused_computation.11 | convolution fusion | flops 1767317504 | bytes 13898752 | tf_op jit(solution)/shard_map/skp,skc->spc/dot_general | solution.py:157
  (21 shorter events, 0.1 us)
Async XLA Ops:
  6.5 2.7 copy-start
  6.5 4.0 %copy-start.3 = (s32[2,16]{1,0:T(2,128)S(1)}, s32[2,16]{1,0:T(2,128)}, u32[]{:S(2)}) copy-start(s32[2,16]{1,0:T(2,128)} %param.12) | copy-start | bytes 388
  6.5 5.4 %copy-start.4 = (s32[2,320]{1,0:T(2,128)S(1)}, s32[2,320]{1,0:T(2,128)}, u32[]{:S(2)}) copy-start(s32[2,320]{1,0:T(2,128)} %param.11) | copy-start | bytes 7684
  6.5 152.0 %all-gather.3.cloned.1.call-start = ((), (), s32[]{:S(2)}) async-start(), calls=%async_computation.5 | async-start | bytes 22282240 | tf_op jit(solution)/shard_map/all_gather | solution.py:52
  9.2 284.7 %all-gather.5.cloned.1.call-start = ((), (), s32[]{:S(2)}) async-start(), calls=%async_computation.6 | async-start | bytes 17825792 | tf_op jit(solution)/shard_map/all_gather | solution.py:53
  18.4 42.1 %all-to-all-start = ((bf16[2,16,20,1024]{3,0,2,1:T(2,128)(2,1)}), bf16[2,16,20,1024]{3,0,2,1:T(2,128)(2,1)S(1)}, u32[]{:S(2)}, u32[]{:S(2)}) async-start(bf16[2,16,20,1024]{3,0,2,1:T(2,128)(2,1)} %bitcast), calls=%async_computation | async-start | bytes 2621440 | tf_op jit(solution)/shard_map/all_to_all | solution.py:68
  125.2 33.4 %copy-start.5 = (f32[8192]{0:T(1024)S(1)}, f32[8192]{0:T(1024)}, u32[]{:S(2)}) copy-start(f32[8192]{0:T(1024)} %param.15) | copy-start | bytes 98308
  172.1 7.2 %copy-start.2 = (s32[2,16,16]{2,1,0:T(8,128)S(1)}, s32[2,16,16]{2,1,0:T(8,128)}, u32[]{:S(2)}) copy-start(s32[2,16,16]{2,1,0:T(8,128)} %param.13) | copy-start | bytes 6148
  173.8 46.4 %all-to-all-start.2 = ((bf16[16,2,128,256]{3,2,1,0:T(8,128)(2,1)}), bf16[16,2,128,256]{3,2,1,0:T(8,128)(2,1)S(1)}, u32[]{:S(2)}, u32[]{:S(2)}) async-start(bf16[16,2,128,256]{3,2,1,0:T(8,128)(2,1)} %broadcast_in_dim.64), calls=%async_computation.2 | async-start | bytes 4194304 | tf_op jit(solution)/shard_map/all_to_all | solution.py:33
  179.0 162.6 %reduce-scatter.2.cloned.1.call-start = ((), (), s32[]{:S(2)}) async-start(), calls=%async_computation.7 | async-start | bytes 4718592 | tf_op jit(solution)/shard_map/reduce_scatter | solution.py:132
  303.6 0.7 copy-start.1
Sparse Core Ops, SparseCore 0:
  9.5 149.0 all-gather.2
  160.7 133.1 all-gather.4
  303.8 37.8 reduce-scatter.1

commit v4 on v3

--- a/solution.py
+++ b/solution.py
@@ -48,8 +48,10 @@
     in_rows, q_cols = w_query.shape
     kv_cols = w_key.shape[1]
     qkv_cols = q_cols + 2 * kv_cols
-    packed = jnp.concatenate([w_query, w_key, w_value], axis=1)
-    w_qkv = lax.all_gather(packed, "fsdp", axis=0, tiled=True)
+    w_q_full = lax.all_gather(w_query, "fsdp", axis=0, tiled=True)
+    w_kv_full = gather_all(jnp.concatenate([w_key, w_value], axis=1), "fsdp", fsdp_size).reshape(
+        fsdp_size * in_rows, 2 * kv_cols
+    )
     w_out_t = lax.all_gather(w_out.T, "fsdp", axis=0, tiled=True)
 
     starts = jnp.cumsum(keep_count, axis=1) - keep_count
@@ -87,12 +89,13 @@
     wide = flat_rows.astype(jnp.float32)
     mean_square = jnp.mean(wide * wide, axis=1, keepdims=True)
     normed = (wide * lax.rsqrt(mean_square + epsilon) * norm_gain).astype(jnp.bfloat16)
-    qkv_sum = jnp.dot(normed, w_qkv, preferred_element_type=jnp.float32).astype(jnp.bfloat16)
+    q_sum = jnp.dot(normed, w_q_full, preferred_element_type=jnp.float32).astype(jnp.bfloat16)
+    kv_sum = jnp.dot(normed, w_kv_full, preferred_element_type=jnp.float32).astype(jnp.bfloat16)
     local_kv = kv_cols // HD
     local_heads = q_cols // HD
     group_size = local_heads // local_kv
-    queries = qkv_sum[:, :q_cols].reshape(seq_count, own_rows, local_kv, group_size, HD)
-    kv_rows = qkv_sum[:, q_cols:].reshape(seq_count, own_rows, 2 * kv_cols)
+    queries = q_sum.reshape(seq_count, own_rows, local_kv, group_size, HD)
+    kv_rows = kv_sum.reshape(seq_count, own_rows, 2 * kv_cols)
     kv_parts = gather_all(kv_rows, "fsdp", fsdp_size)
     keep_total = fsdp_size * own_rows
     all_kv = jnp.transpose(kv_parts, (1, 0, 2, 3)).reshape(seq_count, keep_total, 2 * kv_cols)

time: 382 us -> 409 us (1.071); the launches traced: 382 us -> 404 us
  blocking collectives: 78.6 us -> 23.7 us
  waiting for transfers between devices: 201 us -> 246 us
  local copies, waits for them, and re-layouts: 19.8 us -> 36.4 us
  starting transfers between devices: 12.7 us -> 21.9 us
    all_to_all x1 -> x3, waiting for transfers between devices: 37 us -> 132 us  [gather_all(): lax.all_to_all(copies, axis_name, split_axis=0, concat_axis=0, tiled=True)]
    all_to_all x1 -> x0, blocking collectives: 54.8 us -> none  [gather_all(): lax.all_to_all(copies, axis_name, split_axis=0, concat_axis=0, tiled=True)]
    all_gather x1, waiting for transfers between devices: 32.5 us -> 0.01 us  [shards(): w_q_full = lax.all_gather(w_query, 'fsdp', axis=0, tiled=True)]
    all_gather x1, waiting for transfers between devices: 62.5 us -> 46.3 us  [shards(): w_out_t = lax.all_gather(w_out.T, 'fsdp', axis=0, tiled=True)]
    all_to_all x1 -> x3, starting transfers between devices: 5.26 us -> 14.5 us  [gather_all(): lax.all_to_all(copies, axis_name, split_axis=0, concat_axis=0, tiled=True)]
    unnamed x17 -> x21, local copies, waits for them, and re-layouts: 8.54 us -> 15.8 us
    broadcast_in_dim x2 -> x3, local copies, waits for them, and re-layouts: 2.12 us -> 6.41 us  [gather_all(): copies = jnp.broadcast_to(x[None], (count,) + x.shape)]
    dot_general x1 -> x2, matrix products: 13.6 us -> 16.8 us  [the longest x1 12 us: shards(): jnp.dot(normed, w_q_full, preferred_element_type=jnp.float32)]
  transfers between devices with their start and end apart: 5 -> 7, of which waited for: 5 -> 6; matrix products, arithmetic and copies ran while one was open for 14% -> 19% of each run, Pallas kernels for 0% -> 0%
where the time goes in v4:
time: 409 us; the launch traced here: 404 us
  waiting for transfers between devices  246 us (60%)
  matrix products  50.5 us (12%)
  local copies, waits for them, and re-layouts  36.4 us (9%)
  blocking collectives  23.7 us (6%)
  starting transfers between devices  21.9 us (5%)
  between operations  13.6 us (3%)
  other arithmetic  11.9 us (3%)
    all_to_all x3, waiting for transfers between devices, gather_all(): lax.all_to_all(copies, axis_name, split_axis=0, concat_axis=0, tiled=True)  132 us
    all_gather x1, waiting for transfers between devices, shards(): w_out_t = lax.all_gather(w_out.T, 'fsdp', axis=0, tiled=True)  46.3 us
    reduce_scatter x1, waiting for transfers between devices, shards(): lax.psum_scatter(partial_value.reshape(seq_count, own_rows, full_width).a...  33.9 us
    all_to_all x1, waiting for transfers between devices, shards(): lax.all_to_all(send_rows, 'fsdp', split_axis=1, concat_axis=1, tiled=True)  33.1 us
    all_to_all x1, blocking collectives, shards(): lax.all_to_all(back_rows, 'fsdp', split_axis=1, concat_axis=1, tiled=True)  23.7 us
    unnamed x21, local copies, waits for them, and re-layouts  15.8 us
    all_to_all x3, starting transfers between devices, gather_all(): lax.all_to_all(copies, axis_name, split_axis=0, concat_axis=0, tiled=True)  14.5 us
    dot_general x1, matrix products, shards(): jnp.dot(normed, w_q_full, preferred_element_type=jnp.float32)  12 us
  transfers between devices with their start and end apart: 7, of which 6 were waited for; matrix products, arithmetic and copies ran while one was open for 19% of the time, Pallas kernels for 0%

profile of v4, /device:TPU:0, one launch (start us, length us, event | category | flops | bytes accessed | tf_op | source)
XLA Modules:
  0.0 403.9 jit_solution(541327870809245223)
XLA Ops:
  6.5 0.7 all-gather.3.cloned.1.call-update
  7.3 0.0 all-gather.5.cloned.1.call-start
  7.3 2.3 copy.46
  9.6 0.0 all-gather.5.cloned.1.call-update
  9.6 0.2 reduce_window_sum.11
  9.8 0.2 dynamic-slice_reduce_fusion
  10.0 0.1 and_select_fusion.3
  10.1 0.1 add.259
  10.2 0.1 add.260
  10.3 0.1 add.249
  10.4 0.1 add.252
  10.5 0.1 add.253
  10.6 0.1 add.246
  10.6 0.1 add.247
  10.7 0.1 lt.92
  10.8 0.1 lt.93
  10.9 0.3 select_reduce_fusion
  11.2 0.1 compare_select_fusion.3
  11.3 3.8 fusion.20
  15.1 2.4 copy.36
  17.5 7.1 %all-to-all-start = ((bf16[2,16,20,1024]{3,0,2,1:T(2,128)(2,1)}), bf16[2,16,20,1024]{3,0,2,1:T(2,128)(2,1)S(1)}, u32[]{:S(2)}, u32[]{:S(2)}) async-start(bf16[2,16,20,1024]{3,0,2,1:T(2,128)(2,1)} %bitcast), calls=%async_computation | async-start | bytes 2621440 | tf_op jit(solution)/shard_map/all_to_all | solution.py:70
  24.6 0.1 convert_reduce_fusion
  24.7 0.1 select_reduce_fusion.1
  24.8 33.1 %all-to-all-done = bf16[2,16,20,1024]{3,0,2,1:T(2,128)(2,1)S(1)} async-done(((bf16[2,16,20,1024]{3,0,2,1:T(2,128)(2,1)}), bf16[2,16,20,1024]{3,0,2,1:T(2,128)(2,1)S(1)}, u32[]{:S(2)}, u32[]{:S(2)}) %all-to-all-start) | async-done | bytes 1310752 | tf_op jit(solution)/shard_map/all_to_all | solution.py:70
  57.9 0.6 fusion.30
  58.5 2.6 broadcast_in_dim.64
  61.1 5.4 %all-to-all-start.1 = ((bf16[8,2,128,1024]{3,2,1,0:T(8,128)(2,1)}), bf16[8,2,128,1024]{3,2,1,0:T(8,128)(2,1)}, u32[]{:S(2)}, u32[]{:S(2)}) async-start(bf16[8,2,128,1024]{3,2,1,0:T(8,128)(2,1)} %broadcast_in_dim.64), calls=%async_computation.1 | async-start | bytes 8388608 | tf_op jit(solution)/shard_map/all_to_all | solution.py:33
  66.6 49.7 %all-to-all-done.1 = bf16[8,2,128,1024]{3,2,1,0:T(8,128)(2,1)} async-done(((bf16[8,2,128,1024]{3,2,1,0:T(8,128)(2,1)}), bf16[8,2,128,1024]{3,2,1,0:T(8,128)(2,1)}, u32[]{:S(2)}, u32[]{:S(2)}) %all-to-all-start.1) | async-done | bytes 4194336 | tf_op jit(solution)/shard_map/all_to_all | solution.py:33
  116.3 2.3 broadcast_in_dim.65
  118.6 5.2 %all-to-all-start.2 = ((bf16[16,512,256]{2,1,0:T(8,128)(2,1)}), bf16[16,512,256]{2,1,0:T(8,128)(2,1)}, u32[]{:S(2)}, u32[]{:S(2)}) async-start(bf16[16,512,256]{2,1,0:T(8,128)(2,1)} %broadcast_in_dim.65), calls=%async_computation.2 | async-start | bytes 8388608 | tf_op jit(solution)/shard_map/all_to_all | solution.py:33
  123.8 3.1 fusion.8
  126.9 3.6 fusion.10
  130.5 2.3 copy.39
  132.8 6.3 %copy.57 = bf16[32,8,8,1024]{3,1,2,0:T(8,128)(2,1)} copy(bf16[32,8,8,1024]{3,2,1,0:T(8,128)(2,1)S(1)} %bitcast.104) | data formatting | bytes 8388608
  139.2 56.2 %all-to-all-done.2 = bf16[16,512,256]{2,1,0:T(8,128)(2,1)} async-done(((bf16[16,512,256]{2,1,0:T(8,128)(2,1)}), bf16[16,512,256]{2,1,0:T(8,128)(2,1)}, u32[]{:S(2)}, u32[]{:S(2)}) %all-to-all-start.2) | async-done | bytes 4194336 | tf_op jit(solution)/shard_map/all_to_all | solution.py:33
  195.4 4.7 %convolution_convert_fusion.2 = bf16[256,256]{1,0:T(8,128)(2,1)S(1)} fusion(bf16[256,8192]{1,0:T(8,128)(2,1)} %bitcast.108, bf16[8192,256]{1,0:T(8,128)(2,1)} %bitcast.5), kind=kOutput, calls=%fused_computation.38 | convolution fusion | flops 1073807360 | bytes 8519680 | tf_op jit(solution)/shard_map/dot_general | solution.py:93
  200.1 0.0 copy-start.5
  200.1 1.5 broadcast_in_dim.67
  201.7 3.9 all-to-all-start.3
  205.6 0.2 reduce-scatter.2.cloned.1.call-start
  205.8 0.1 copy.41
  205.9 0.1 fusion.58
  206.1 0.2 broadcast_compare_fusion
  206.3 0.6 fusion.19
  206.9 1.0 copy.42
  207.9 4.6 %copy.38 = bf16[2,128,8,1024]{3,2,1,0:T(8,128)(2,1)S(1)} copy(bf16[2,128,8,1024]{3,1,0,2:T(8,128)(2,1)} %bitcast.2) | data formatting | bytes 8388608 | tf_op jit(solution)/shard_map/transpose | solution.py:81
  212.5 6.3 %copy.56 = bf16[32,8,8,1024]{3,1,2,0:T(8,128)(2,1)} copy(bf16[32,8,8,1024]{3,2,1,0:T(8,128)(2,1)S(1)} %bitcast.105) | data formatting | bytes 8388608
  218.8 25.9 %all-to-all-done.3 = bf16[16,2,128,256]{3,2,1,0:T(8,128)(2,1)S(1)} async-done(((bf16[16,2,128,256]{3,2,1,0:T(8,128)(2,1)}), bf16[16,2,128,256]{3,2,1,0:T(8,128)(2,1)S(1)}, u32[]{:S(2)}, u32[]{:S(2)}) %all-to-all-start.3) | async-done | bytes 2097184 | tf_op jit(solution)/shard_map/all_to_all | solution.py:33
  244.7 1.5 copy.40
  246.3 12.0 %fusion.33 = bf16[32,8,8,128]{3,1,2,0:T(8,128)(2,1)S(1)} fusion(bf16[8192,1024]{1,0:T(8,128)(2,1)} %all-gather.3.cloned.1.call-done, bf16[256,8192]{1,0:T(8,128)(2,1)} %bitcast.102, f32[8192]{0:T(1024)S(1)} %copy-done.3, f32[256]{0:T(256)S(1)} %get-tuple-element.9), kind=kOutput, calls=%fused_computation.37 | convolution fusion | flops 4303618048 | bytes 21529600 | tf_op jit(solution)/shard_map/dot_general | solution.py:92
  258.3 0.1 copy.58
  258.4 2.9 fusion.2
  261.4 4.1 %fusion.3 = f32[2,8,128]{2,1,0:T(8,128)S(1)} fusion(f32[2,2048,128,8]{2,1,3,0:T(8,128)S(1)} %get-tuple-element.14, f32[2,8,128]{2,1,0:T(8,128)S(1)} %get-tuple-element.13, pred[2,128,2048]{1,2,0:T(8,128)(4,1)S(1)} %copy.42), kind=kLoop, calls=%fused_computation.5 | loop fusion | flops 20969472 | bytes 17317888 | tf_op jit(solution)/shard_map/reduce_sum | solution.py:120
  265.4 4.2 %divide_convert_fusion = bf16[2,128,1,8,128]{1,4,3,0,2:T(8,128)(2,1)S(1)} fusion(f32[2,2048,128,8]{2,1,3,0:T(8,128)S(1)} %get-tuple-element.14, f32[2,8,128]{2,1,0:T(8,128)S(1)} %get-tuple-element.13, pred[2,128,2048]{1,2,0:T(8,128)(4,1)S(1)} %copy.42, bf16[2,2048,256]{2,1,0:T(8,128)(2,1)S(1)} %bitcast.111, f32[2,128,8]{1,2,0:T(8,128)S(1)} %bitcast.118), kind=kOutput, calls=%fused_computation.43 | convolution fusion | flops 1095237632 | bytes 18890752 | tf_op jit(solution)/shard_map/skgqt,stkd->sqkgd/dot_general | solution.py:121
  269.7 46.3 %all-gather.5.cloned.1.call-done = bf16[8192,1024]{1,0:T(8,128)(2,1)} async-done(((bf16[512,1024]{1,0:T(8,128)(2,1)}), bf16[8192,1024]{1,0:T(8,128)(2,1)}) %all-gather.5.cloned.1.call-update) | async-done | bytes 16777232 | tf_op jit(solution)/shard_map/all_gather | solution.py:55
  315.9 9.5 %fusion.5 = bf16[2,128,8192]{2,1,0:T(8,128)(2,1)} fusion(bf16[2,128,1024]{1,2,0:T(8,128)(2,1)S(1)} %bitcast.120, bf16[8192,1024]{1,0:T(8,128)(2,1)} %all-gather.5.cloned.1.call-done), kind=kOutput, calls=%fused_computation.9 | convolution fusion | flops 4297064448 | bytes 21495808 | tf_op jit(solution)/shard_map/rk,nk->rn/dot_general | solution.py:132
  325.4 0.0 reduce-scatter.2.cloned.1.call-update
  325.5 0.7 copy-done.4
  326.2 3.4 fusion.76
  329.6 33.9 %reduce-scatter.2.cloned.1.call-done = bf16[2,128,1024]{2,1,0:T(8,128)(2,1)} async-done(((bf16[2,128,8192]{2,1,0:T(8,128)(2,1)}), bf16[2,128,1024]{2,1,0:T(8,128)(2,1)}) %reduce-scatter.2.cloned.1.call-update) | async-done | bytes 524304 | tf_op jit(solution)/shard_map/reduce_scatter | solution.py:135
  363.4 1.6 convolution_convert_fusion.1
  365.0 1.3 copy.48
  366.4 23.7 %all_to_all.25 = bf16[2,16,20,1024]{3,0,2,1:T(2,128)(2,1)S(1)} all-to-all(bf16[2,16,20,1024]{3,0,2,1:T(2,128)(2,1)S(1)} %bitcast.107), channel_id=1, replica_groups=mesh['seq'=8,'fsdp'=16] {'fsdp'}, dimensions={1} | all-to-all | bytes 2621440 | tf_op jit(solution)/shard_map/all_to_all | solution.py:151
  390.2 7.0 %convert_add_fusion = f32[2,1024,1024]{2,1,0:T(8,128)} fusion(bf16[2,1024,1024]{2,1,0:T(8,128)(2,1)} %param.10, s32[2,320]{1,0:T(2,128)S(1)} %get-tuple-element.12, bf16[2,320,1024]{2,0,1:T(2,128)(2,1)S(1)} %bitcast.113, s32[2,320]{1,0:T(2,128)S(1)} %get-tuple-element.11), kind=kOutput, calls=%fused_computation.15 | convolution fusion | flops 1767317504 | bytes 13898752 | tf_op jit(solution)/shard_map/skp,skc->spc/dot_general | solution.py:160
  (32 shorter events, 0.2 us)
Async XLA Ops:
  6.5 3.1 copy-start.6
  6.5 4.4 %copy-start.7 = (s32[2,320]{1,0:T(2,128)S(1)}, s32[2,320]{1,0:T(2,128)}, u32[]{:S(2)}) copy-start(s32[2,320]{1,0:T(2,128)} %param.11) | copy-start | bytes 7684
  6.5 239.7 %all-gather.3.cloned.1.call-start = ((), (), s32[]{:S(2)}) async-start(), calls=%async_computation.6 | async-start | bytes 17825792 | tf_op jit(solution)/shard_map/all_gather | solution.py:51
  7.3 308.7 %all-gather.5.cloned.1.call-start = ((), (), s32[]{:S(2)}) async-start(), calls=%async_computation.7 | async-start | bytes 17825792 | tf_op jit(solution)/shard_map/all_gather | solution.py:55
  17.5 40.5 %all-to-all-start = ((bf16[2,16,20,1024]{3,0,2,1:T(2,128)(2,1)}), bf16[2,16,20,1024]{3,0,2,1:T(2,128)(2,1)S(1)}, u32[]{:S(2)}, u32[]{:S(2)}) async-start(bf16[2,16,20,1024]{3,0,2,1:T(2,128)(2,1)} %bitcast), calls=%async_computation | async-start | bytes 2621440 | tf_op jit(solution)/shard_map/all_to_all | solution.py:70
  61.1 5.4 %copy-start.1 = (bf16[512,128]{1,0:T(8,128)(2,1)S(1)}, bf16[512,128]{1,0:T(8,128)(2,1)}, u32[]{:S(2)}) copy-start(bf16[512,128]{1,0:T(8,128)(2,1)} %param.18) | copy-start | bytes 393220
  61.1 5.4 %copy-start.2 = (bf16[512,128]{1,0:T(8,128)(2,1)S(1)}, bf16[512,128]{1,0:T(8,128)(2,1)}, u32[]{:S(2)}) copy-start(bf16[512,128]{1,0:T(8,128)(2,1)} %param.17) | copy-start | bytes 393220
  61.1 55.2 %all-to-all-start.1 = ((bf16[8,2,128,1024]{3,2,1,0:T(8,128)(2,1)}), bf16[8,2,128,1024]{3,2,1,0:T(8,128)(2,1)}, u32[]{:S(2)}, u32[]{:S(2)}) async-start(bf16[8,2,128,1024]{3,2,1,0:T(8,128)(2,1)} %broadcast_in_dim.64), calls=%async_computation.1 | async-start | bytes 8388608 | tf_op jit(solution)/shard_map/all_to_all | solution.py:33
  118.6 5.2 %copy-start.3 = (f32[8192]{0:T(1024)S(1)}, f32[8192]{0:T(1024)}, u32[]{:S(2)}) copy-start(f32[8192]{0:T(1024)} %param.15) | copy-start | bytes 98308
  118.6 76.8 %all-to-all-start.2 = ((bf16[16,512,256]{2,1,0:T(8,128)(2,1)}), bf16[16,512,256]{2,1,0:T(8,128)(2,1)}, u32[]{:S(2)}, u32[]{:S(2)}) async-start(bf16[16,512,256]{2,1,0:T(8,128)(2,1)} %broadcast_in_dim.65), calls=%async_computation.2 | async-start | bytes 8388608 | tf_op jit(solution)/shard_map/all_to_all | solution.py:33
  200.1 5.7 %copy-start.5 = (s32[2,16,16]{2,1,0:T(8,128)S(1)}, s32[2,16,16]{2,1,0:T(8,128)}, u32[]{:S(2)}) copy-start(s32[2,16,16]{2,1,0:T(8,128)} %param.13) | copy-start | bytes 6148
  201.7 43.1 %all-to-all-start.3 = ((bf16[16,2,128,256]{3,2,1,0:T(8,128)(2,1)}), bf16[16,2,128,256]{3,2,1,0:T(8,128)(2,1)S(1)}, u32[]{:S(2)}, u32[]{:S(2)}) async-start(bf16[16,2,128,256]{3,2,1,0:T(8,128)(2,1)} %broadcast_in_dim.67), calls=%async_computation.3 | async-start | bytes 4194304 | tf_op jit(solution)/shard_map/all_to_all | solution.py:33
  205.6 157.9 %reduce-scatter.2.cloned.1.call-start = ((), (), s32[]{:S(2)}) async-start(), calls=%async_computation.8 | async-start | bytes 4718592 | tf_op jit(solution)/shard_map/reduce_scatter | solution.py:135
  246.3 12.1 %copy-start = (bf16[2,16,128,256]{3,2,1,0:T(8,128)(2,1)S(1)}, bf16[2,16,128,256]{3,2,1,0:T(8,128)(2,1)}, u32[]{:S(2)}) copy-start(bf16[2,16,128,256]{3,2,1,0:T(8,128)(2,1)} %copy.40) | copy-start | bytes 6291460
  325.4 0.7 copy-start.4
Sparse Core Ops, SparseCore 0:
  9.5 164.5 all-gather.2
  176.2 139.7 all-gather.4
  325.6 37.7 reduce-scatter.1

commit v5 on v3

--- a/solution.py
+++ b/solution.py
@@ -127,14 +127,14 @@
         .reshape(row_total, local_heads * HD)
     )
     partial_value = jnp.einsum(
-        "rk,nk->rn", attended, w_out_t, preferred_element_type=jnp.float32
+        "rk,jck->jrc",
+        attended,
+        w_out_t.reshape(seq_size, part_width, local_heads * HD),
+        preferred_element_type=jnp.float32,
     )
     summed = lax.psum_scatter(
-        partial_value.reshape(seq_count, own_rows, full_width).astype(jnp.bfloat16),
-        "seq",
-        scatter_dimension=2,
-        tiled=True,
-    ).astype(jnp.float32)
+        partial_value.astype(jnp.bfloat16), "seq", scatter_dimension=0, tiled=True
+    ).reshape(seq_count, own_rows, part_width).astype(jnp.float32)
     update = (gate_value.reshape(seq_count, own_rows, 1) * summed).astype(jnp.bfloat16)
 
     first_back = jnp.mod(owner_idx - starts, fsdp_size)[:, :, None]

time: 382 us -> 426 us (1.12)
  local copies, waits for them, and re-layouts: 19.8 us -> 41.5 us
  waiting for transfers between devices: 201 us -> 222 us
    all_gather x1, waiting for transfers between devices: 62.5 us -> 119 us  [shards(): w_out_t = lax.all_gather(w_out.T, 'fsdp', axis=0, tiled=True)]
    all_to_all x1, waiting for transfers between devices: 37 us -> 0.01 us  [gather_all(): lax.all_to_all(copies, axis_name, split_axis=0, concat_axis=0, tiled=True)]
    all_gather x0 -> x1, local copies, waits for them, and re-layouts: none -> 22.4 us  [shards(): w_out_t = lax.all_gather(w_out.T, 'fsdp', axis=0, tiled=True)]
    unnamed x17 -> x14, local copies, waits for them, and re-layouts: 8.54 us -> 7.22 us
  transfers between devices with their start and end apart: 5 -> 5, of which waited for: 5 -> 4; matrix products, arithmetic and copies ran while one was open for 14% -> 15% of each run, Pallas kernels for 0% -> 0%
where the time goes in v5:
time: 426 us; the launch traced here: 425 us
  waiting for transfers between devices  222 us (52%)
  blocking collectives  78.5 us (18%)
  matrix products  48 us (11%)
  local copies, waits for them, and re-layouts  41.5 us (10%)
  between operations  13.4 us (3%)
  starting transfers between devices  12.7 us (3%)
  other arithmetic  8.66 us (2%)
    all_gather x1, waiting for transfers between devices, shards(): w_out_t = lax.all_gather(w_out.T, 'fsdp', axis=0, tiled=True)  119 us
    all_to_all x1, blocking collectives, gather_all(): lax.all_to_all(copies, axis_name, split_axis=0, concat_axis=0, tiled=True)  54.8 us
    all_to_all x1, waiting for transfers between devices, shards(): lax.all_to_all(send_rows, 'fsdp', split_axis=1, concat_axis=1, tiled=True)  34.7 us
    reduce_scatter x1, waiting for transfers between devices, shards(): lax.psum_scatter(partial_value.astype(jnp.bfloat16), 'seq', scatter_dimen...  33.6 us
    all_gather x1, waiting for transfers between devices, shards(): w_qkv = lax.all_gather(packed, 'fsdp', axis=0, tiled=True)  33.2 us
    all_to_all x1, blocking collectives, shards(): lax.all_to_all(back_rows, 'fsdp', split_axis=1, concat_axis=1, tiled=True)  23.7 us
    all_gather x1, local copies, waits for them, and re-layouts, shards(): w_out_t = lax.all_gather(w_out.T, 'fsdp', axis=0, tiled=True)  22.4 us
    dot_general x1, matrix products, shards(): jnp.dot(normed, w_qkv, preferred_element_type=jnp.float32)  13.6 us
  transfers between devices with their start and end apart: 5, of which 4 were waited for; matrix products, arithmetic and copies ran while one was open for 15% of the time, Pallas kernels for 0%

profile of v5, /device:TPU:0, one launch (start us, length us, event | category | flops | bytes accessed | tf_op | source)
XLA Modules:
  0.0 424.6 jit_solution(6292329360062802899)
XLA Ops:
  6.5 0.0 all-gather.3.cloned.1.call-start
  6.5 2.6 pad_maximum_fusion
  9.1 0.0 all-gather.3.cloned.1.call-update
  9.1 0.0 all-gather.5.cloned.1.call-start
  9.2 0.7 all-gather.5.cloned.1.call-update
  9.9 0.0 copy-done.2
  9.9 0.2 reduce_window_sum.11
  10.1 0.2 dynamic-slice_reduce_fusion
  10.3 0.1 and_select_fusion.3
  10.4 0.1 add.258
  10.5 0.1 add.259
  10.6 0.1 add.248
  10.7 0.1 add.251
  10.7 0.1 add.252
  10.8 0.1 add.245
  10.9 0.1 add.246
  11.0 0.1 lt.92
  11.1 0.1 lt.93
  11.2 0.0 copy-done.3
  11.2 0.3 select_reduce_fusion
  11.5 0.1 compare_select_fusion.3
  11.6 3.8 fusion.13
  15.3 2.4 copy.38
  17.7 7.1 %all-to-all-start = ((bf16[2,16,20,1024]{3,0,2,1:T(2,128)(2,1)}), bf16[2,16,20,1024]{3,0,2,1:T(2,128)(2,1)S(1)}, u32[]{:S(2)}, u32[]{:S(2)}) async-start(bf16[2,16,20,1024]{3,0,2,1:T(2,128)(2,1)} %bitcast), calls=%async_computation | async-start | bytes 2621440 | tf_op jit(solution)/shard_map/all_to_all | solution.py:68
  24.9 0.1 convert_reduce_fusion
  25.0 0.1 select_reduce_fusion.1
  25.1 34.7 %all-to-all-done = bf16[2,16,20,1024]{3,0,2,1:T(2,128)(2,1)S(1)} async-done(((bf16[2,16,20,1024]{3,0,2,1:T(2,128)(2,1)}), bf16[2,16,20,1024]{3,0,2,1:T(2,128)(2,1)S(1)}, u32[]{:S(2)}, u32[]{:S(2)}) %all-to-all-start) | async-done | bytes 1310752 | tf_op jit(solution)/shard_map/all_to_all | solution.py:68
  59.8 0.6 fusion.22
  60.4 0.5 broadcast_in_dim.62
  61.0 54.8 %all_to_all.20 = bf16[8,2,128,1024]{3,2,1,0:T(8,128)(2,1)S(1)} all-to-all(bf16[8,2,128,1024]{3,2,1,0:T(8,128)(2,1)S(1)} %broadcast_in_dim.62), channel_id=1, replica_groups=mesh['seq'=8,'fsdp'=16] {'seq'}, dimensions={0} | all-to-all | bytes 8388608 | tf_op jit(solution)/shard_map/all_to_all | solution.py:33
  115.8 2.3 copy.40
  118.1 6.3 %copy.56 = bf16[32,8,8,1024]{3,1,2,0:T(8,128)(2,1)} copy(bf16[32,8,8,1024]{3,2,1,0:T(8,128)(2,1)S(1)} %bitcast.103) | data formatting | bytes 8388608
  124.5 0.9 multiply_reduce_fusion
  125.4 33.2 %all-gather.3.cloned.1.call-done = bf16[8192,1280]{1,0:T(8,128)(2,1)} async-done(((bf16[512,1280]{1,0:T(8,128)(2,1)}), bf16[8192,1280]{1,0:T(8,128)(2,1)}) %all-gather.3.cloned.1.call-update) | async-done | bytes 20971536 | tf_op jit(solution)/shard_map/all_gather | solution.py:52
  158.6 13.6 %fusion.11 = bf16[256,1280]{1,0:T(8,128)(2,1)S(1)} fusion(bf16[8192,1280]{1,0:T(8,128)(2,1)} %all-gather.3.cloned.1.call-done, bf16[256,8192]{1,0:T(8,128)(2,1)} %bitcast.101, f32[8192]{0:T(1024)S(1)} %copy-done.4, f32[256]{0:T(256)S(1)} %rsqrt_bitcast_fusion), kind=kOutput, calls=%fused_computation.18 | convolution fusion | flops 5377425408 | bytes 25854976 | tf_op jit(solution)/shard_map/dot_general | solution.py:90
  172.2 0.0 copy-start.1
  172.3 1.6 broadcast_in_dim.64
  173.8 5.3 %all-to-all-start.2 = ((bf16[16,2,128,256]{3,2,1,0:T(8,128)(2,1)}), bf16[16,2,128,256]{3,2,1,0:T(8,128)(2,1)S(1)}, u32[]{:S(2)}, u32[]{:S(2)}) async-start(bf16[16,2,128,256]{3,2,1,0:T(8,128)(2,1)} %broadcast_in_dim.64), calls=%async_computation.2 | async-start | bytes 4194304 | tf_op jit(solution)/shard_map/all_to_all | solution.py:33
  179.1 0.3 reduce-scatter.2.cloned.1.call-start
  179.4 0.1 copy.42
  179.5 0.1 fusion.51
  179.7 0.2 broadcast_compare_fusion
  179.9 1.4 fusion.12
  181.3 1.9 copy.43
  183.2 119.4 %all-gather.5.cloned.1.call-done = bf16[8192,1024]{0,1:T(8,128)(2,1)} async-done(((bf16[512,1024]{0,1:T(8,128)(2,1)}), bf16[8192,1024]{0,1:T(8,128)(2,1)}) %all-gather.5.cloned.1.call-update) | async-done | bytes 16777232 | tf_op jit(solution)/shard_map/all_gather | solution.py:53
  302.6 22.4 %copy.48 = bf16[8192,1024]{1,0:T(8,128)(2,1)} copy(bf16[8192,1024]{0,1:T(8,128)(2,1)} %all-gather.5.cloned.1.call-done) | data formatting | bytes 33554432 | tf_op jit(solution)/shard_map/all_gather | solution.py:53
  325.0 0.1 slice_bitcast_fusion.6
  325.1 0.1 copy.57
  325.2 0.0 all-to-all-done.2
  325.2 0.2 copy.41
  325.4 2.7 fusion
  328.2 4.1 fusion.1
  332.2 4.2 divide_convert_fusion
  336.4 0.3 copy.47
  336.8 0.2 reshape.559
  337.0 9.5 %convert_bitcast_fusion = bf16[8,256,1024]{2,1,0:T(8,128)(2,1)} fusion(bf16[256,1024,1]{1,0,2:T(8,128)(2,1)S(1)} %reshape.559, bf16[8,1024,1024]{2,1,0:T(8,128)(2,1)} %bitcast.100), kind=kOutput, calls=%fused_computation.12 | convolution fusion | flops 4297064448 | bytes 21495808 | tf_op jit(solution)/shard_map/rk,jck->jrc/dot_general | solution.py:129
  346.5 0.0 reduce-scatter.2.cloned.1.call-update
  346.6 0.7 copy-done
  347.3 3.4 fusion.68
  350.7 33.6 %reduce-scatter.2.cloned.1.call-done = bf16[1,256,1024]{2,1,0:T(8,128)(2,1)} async-done(((bf16[8,256,1024]{2,1,0:T(8,128)(2,1)}), bf16[1,256,1024]{2,1,0:T(8,128)(2,1)}) %reduce-scatter.2.cloned.1.call-update) | async-done | bytes 524304 | tf_op jit(solution)/shard_map/reduce_scatter | solution.py:135
  384.3 1.6 convolution_convert_fusion.1
  385.9 1.3 copy.49
  387.3 23.7 %all_to_all.21 = bf16[2,16,20,1024]{3,0,2,1:T(2,128)(2,1)S(1)} all-to-all(bf16[2,16,20,1024]{3,0,2,1:T(2,128)(2,1)S(1)} %bitcast.105), channel_id=1, replica_groups=mesh['seq'=8,'fsdp'=16] {'fsdp'}, dimensions={1} | all-to-all | bytes 2621440 | tf_op jit(solution)/shard_map/all_to_all | solution.py:148
  411.0 7.0 %convert_add_fusion = f32[2,1024,1024]{2,1,0:T(8,128)} fusion(bf16[2,1024,1024]{2,1,0:T(8,128)(2,1)} %param.10, s32[2,320]{1,0:T(2,128)S(1)} %get-tuple-element.10, bf16[2,320,1024]{2,0,1:T(2,128)(2,1)S(1)} %bitcast.109, s32[2,320]{1,0:T(2,128)S(1)} %get-tuple-element.9), kind=kOutput, calls=%fused_computation.8 | convolution fusion | flops 1767317504 | bytes 13898752 | tf_op jit(solution)/shard_map/skp,skc->spc/dot_general | solution.py:157
  (21 shorter events, 0.1 us)
Async XLA Ops:
  6.5 3.3 copy-start.2
  6.5 4.7 %copy-start.3 = (s32[2,320]{1,0:T(2,128)S(1)}, s32[2,320]{1,0:T(2,128)}, u32[]{:S(2)}) copy-start(s32[2,320]{1,0:T(2,128)} %param.11) | copy-start | bytes 7684
  6.5 152.1 %all-gather.3.cloned.1.call-start = ((), (), s32[]{:S(2)}) async-start(), calls=%async_computation.5 | async-start | bytes 22282240 | tf_op jit(solution)/shard_map/all_gather | solution.py:52
  9.1 293.5 %all-gather.5.cloned.1.call-start = ((), (), s32[]{:S(2)}) async-start(), calls=%async_computation.6 | async-start | bytes 17825792 | tf_op jit(solution)/shard_map/all_gather | solution.py:53
  17.7 42.1 %all-to-all-start = ((bf16[2,16,20,1024]{3,0,2,1:T(2,128)(2,1)}), bf16[2,16,20,1024]{3,0,2,1:T(2,128)(2,1)S(1)}, u32[]{:S(2)}, u32[]{:S(2)}) async-start(bf16[2,16,20,1024]{3,0,2,1:T(2,128)(2,1)} %bitcast), calls=%async_computation | async-start | bytes 2621440 | tf_op jit(solution)/shard_map/all_to_all | solution.py:68
  124.5 34.1 %copy-start.4 = (f32[8192]{0:T(1024)S(1)}, f32[8192]{0:T(1024)}, u32[]{:S(2)}) copy-start(f32[8192]{0:T(1024)} %param.15) | copy-start | bytes 98308
  172.2 7.2 %copy-start.1 = (s32[2,16,16]{2,1,0:T(8,128)S(1)}, s32[2,16,16]{2,1,0:T(8,128)}, u32[]{:S(2)}) copy-start(s32[2,16,16]{2,1,0:T(8,128)} %param.13) | copy-start | bytes 6148
  173.8 151.4 %all-to-all-start.2 = ((bf16[16,2,128,256]{3,2,1,0:T(8,128)(2,1)}), bf16[16,2,128,256]{3,2,1,0:T(8,128)(2,1)S(1)}, u32[]{:S(2)}, u32[]{:S(2)}) async-start(bf16[16,2,128,256]{3,2,1,0:T(8,128)(2,1)} %broadcast_in_dim.64), calls=%async_computation.2 | async-start | bytes 4194304 | tf_op jit(solution)/shard_map/all_to_all | solution.py:33
  179.1 205.2 %reduce-scatter.2.cloned.1.call-start = ((), (), s32[]{:S(2)}) async-start(), calls=%async_computation.7 | async-start | bytes 4718592 | tf_op jit(solution)/shard_map/reduce_scatter | solution.py:135
  346.5 0.7 copy-start
Sparse Core Ops, SparseCore 0:
  9.5 149.0 all-gather.2
  160.7 141.8 all-gather.4
  346.7 37.5 reduce-scatter.1

commit v6 on v3

--- a/solution.py
+++ b/solution.py
@@ -75,19 +75,25 @@
     narrow_rows = select_rows(
         flat_index, received.reshape(seq_count, fsdp_size * slot_count, part_width)
     )
-    row_parts = gather_all(narrow_rows, "seq", seq_size)
-    full_rows = jnp.transpose(row_parts, (1, 2, 0, 3)).reshape(
-        seq_count, own_rows, seq_size * part_width
+    row_total = seq_count * own_rows
+    full_width = seq_size * part_width
+    row_parts = gather_all(narrow_rows.reshape(row_total, part_width), "seq", seq_size)
+    router_logit = jnp.einsum(
+        "jrc,jc->r", row_parts, router.reshape(seq_size, part_width),
+        preferred_element_type=jnp.float32,
     )
-    full_width = full_rows.shape[2]
-    row_total = seq_count * own_rows
-    flat_rows = full_rows.reshape(row_total, full_width)
-    router_logit = jnp.dot(flat_rows, router, preferred_element_type=jnp.float32)
     gate_value = jax.nn.sigmoid(router_logit)
-    wide = flat_rows.astype(jnp.float32)
-    mean_square = jnp.mean(wide * wide, axis=1, keepdims=True)
-    normed = (wide * lax.rsqrt(mean_square + epsilon) * norm_gain).astype(jnp.bfloat16)
-    qkv_sum = jnp.dot(normed, w_qkv, preferred_element_type=jnp.float32).astype(jnp.bfloat16)
+    wide = row_parts.astype(jnp.float32)
+    mean_square = jnp.sum(wide * wide, axis=(0, 2)) / full_width
+    normed = (
+        wide
+        * lax.rsqrt(mean_square + epsilon)[None, :, None]
+        * norm_gain.reshape(seq_size, 1, part_width)
+    ).astype(jnp.bfloat16)
+    qkv_sum = jnp.einsum(
+        "jrc,jcn->rn", normed, w_qkv.reshape(seq_size, part_width, qkv_cols),
+        preferred_element_type=jnp.float32,
+    ).astype(jnp.bfloat16)
     local_kv = kv_cols // HD
     local_heads = q_cols // HD
     group_size = local_heads // local_kv

time: 382 us -> 383 us (level)
  waiting for transfers between devices: 201 us -> 256 us
  blocking collectives: 78.6 us -> 23.8 us
  local copies, waits for them, and re-layouts: 19.8 us -> 13.2 us
  starting transfers between devices: 12.7 us -> 18.1 us
    all_to_all x1 -> x0, blocking collectives: 54.8 us -> none  [gather_all(): lax.all_to_all(copies, axis_name, split_axis=0, concat_axis=0, tiled=True)]
    all_to_all x1 -> x2, waiting for transfers between devices: 37 us -> 87.4 us  [gather_all(): lax.all_to_all(copies, axis_name, split_axis=0, concat_axis=0, tiled=True)]
    unnamed x17 -> x15, local copies, waits for them, and re-layouts: 8.54 us -> 2.21 us
    all_to_all x1 -> x2, starting transfers between devices: 5.26 us -> 10.7 us  [gather_all(): lax.all_to_all(copies, axis_name, split_axis=0, concat_axis=0, tiled=True)]
    all_gather x1, waiting for transfers between devices: 32.5 us -> 36.4 us  [shards(): w_qkv = lax.all_gather(packed, 'fsdp', axis=0, tiled=True)]
  transfers between devices with their start and end apart: 5 -> 6, of which waited for: 5 -> 6; matrix products, arithmetic and copies ran while one was open for 14% -> 13% of each run, Pallas kernels for 0% -> 0%
where the time goes in v6:
time: 383 us; the launch traced here: 382 us
  waiting for transfers between devices  256 us (67%)
  matrix products  46.7 us (12%)
  blocking collectives  23.8 us (6%)
  starting transfers between devices  18.1 us (5%)
  between operations  13.4 us (3%)
  local copies, waits for them, and re-layouts  13.2 us (3%)
  other arithmetic  11.1 us (3%)
    all_to_all x2, waiting for transfers between devices, gather_all(): lax.all_to_all(copies, axis_name, split_axis=0, concat_axis=0, tiled=True)  87.4 us
    all_gather x1, waiting for transfers between devices, shards(): w_out_t = lax.all_gather(w_out.T, 'fsdp', axis=0, tiled=True)  63.3 us
    all_gather x1, waiting for transfers between devices, shards(): w_qkv = lax.all_gather(packed, 'fsdp', axis=0, tiled=True)  36.4 us
    all_to_all x1, waiting for transfers between devices, shards(): lax.all_to_all(send_rows, 'fsdp', split_axis=1, concat_axis=1, tiled=True)  34.7 us
    reduce_scatter x1, waiting for transfers between devices, shards(): lax.psum_scatter(partial_value.reshape(seq_count, own_rows, full_width).a...  33.9 us
    all_to_all x1, blocking collectives, shards(): lax.all_to_all(back_rows, 'fsdp', split_axis=1, concat_axis=1, tiled=True)  23.8 us
    dot_general x1, matrix products, shards(): jnp.einsum('jrc,jcn->rn', normed, w_qkv.reshape(seq_size, part_width, qkv...  12.1 us
    all_to_all x2, starting transfers between devices, gather_all(): lax.all_to_all(copies, axis_name, split_axis=0, concat_axis=0, tiled=True)  10.7 us
  transfers between devices with their start and end apart: 6, of which 6 were waited for; matrix products, arithmetic and copies ran while one was open for 13% of the time, Pallas kernels for 0%

profile of v6, /device:TPU:0, one launch (start us, length us, event | category | flops | bytes accessed | tf_op | source)
XLA Modules:
  0.0 382.0 jit_solution(14112750524147153284)
XLA Ops:
  6.5 0.0 all-gather.3.cloned.1.call-start
  6.5 2.6 pad_maximum_fusion
  9.2 0.0 all-gather.3.cloned.1.call-update
  9.2 0.0 all-gather.5.cloned.1.call-start
  9.2 0.0 copy-done
  9.2 1.3 copy.42
  10.6 0.0 all-gather.5.cloned.1.call-update
  10.6 0.0 copy-done.4
  10.6 0.2 reduce_window_sum.11
  10.8 0.2 dynamic-slice_reduce_fusion
  11.1 0.1 and_select_fusion.3
  11.1 0.1 add.256
  11.2 0.1 add.257
  11.3 0.1 add.246
  11.4 0.1 add.249
  11.5 0.1 add.250
  11.6 0.1 add.243
  11.7 0.1 add.244
  11.7 0.1 lt.92
  11.8 0.1 lt.93
  11.9 0.0 copy-done.5
  11.9 0.3 select_reduce_fusion
  12.2 0.1 compare_select_fusion.3
  12.3 3.8 fusion.27
  16.1 2.4 copy.34
  18.5 7.1 %all-to-all-start = ((bf16[2,16,20,1024]{3,0,2,1:T(2,128)(2,1)}), bf16[2,16,20,1024]{3,0,2,1:T(2,128)(2,1)S(1)}, u32[]{:S(2)}, u32[]{:S(2)}) async-start(bf16[2,16,20,1024]{3,0,2,1:T(2,128)(2,1)} %bitcast), calls=%async_computation | async-start | bytes 2621440 | tf_op jit(solution)/shard_map/all_to_all | solution.py:68
  25.7 0.1 convert_reduce_fusion
  25.7 0.1 select_reduce_fusion.1
  25.8 34.7 %all-to-all-done = bf16[2,16,20,1024]{3,0,2,1:T(2,128)(2,1)S(1)} async-done(((bf16[2,16,20,1024]{3,0,2,1:T(2,128)(2,1)}), bf16[2,16,20,1024]{3,0,2,1:T(2,128)(2,1)S(1)}, u32[]{:S(2)}, u32[]{:S(2)}) %all-to-all-start) | async-done | bytes 1310752 | tf_op jit(solution)/shard_map/all_to_all | solution.py:68
  60.6 0.6 fusion.36
  61.2 2.6 broadcast_in_dim.65
  63.7 5.5 %all-to-all-start.1 = ((bf16[8,256,1024]{2,1,0:T(8,128)(2,1)}), bf16[8,256,1024]{2,1,0:T(8,128)(2,1)}, u32[]{:S(2)}, u32[]{:S(2)}) async-start(bf16[8,256,1024]{2,1,0:T(8,128)(2,1)} %broadcast_in_dim.65), calls=%async_computation.1 | async-start | bytes 8388608 | tf_op jit(solution)/shard_map/all_to_all | solution.py:33
  69.2 0.0 copy-done.1
  69.2 49.7 %all-to-all-done.1 = bf16[8,256,1024]{2,1,0:T(8,128)(2,1)} async-done(((bf16[8,256,1024]{2,1,0:T(8,128)(2,1)}), bf16[8,256,1024]{2,1,0:T(8,128)(2,1)}, u32[]{:S(2)}, u32[]{:S(2)}) %all-to-all-start.1) | async-done | bytes 4194336 | tf_op jit(solution)/shard_map/all_to_all | solution.py:33
  118.9 3.3 fusion.8
  122.2 36.4 %all-gather.3.cloned.1.call-done = bf16[8192,1280]{1,0:T(8,128)(2,1)} async-done(((bf16[512,1280]{1,0:T(8,128)(2,1)}), bf16[8192,1280]{1,0:T(8,128)(2,1)}) %all-gather.3.cloned.1.call-update) | async-done | bytes 20971536 | tf_op jit(solution)/shard_map/all_gather | solution.py:52
  158.6 12.1 %fusion.23 = bf16[256,1280]{1,0:T(8,128)(2,1)S(1)} fusion(bf16[8,1024,1280]{2,1,0:T(8,128)(2,1)} %bitcast.108, bf16[8,256,1024]{2,1,0:T(8,128)(2,1)} %all-to-all-done.1, f32[8,1024]{1,0:T(8,128)S(1)} %mul.118, f32[256]{0:T(256)S(1)} %add_rsqrt_fusion), kind=kOutput, calls=%fused_computation.24 | convolution fusion | flops 5377425408 | bytes 25854976 | tf_op jit(solution)/shard_map/jrc,jcn->rn/dot_general | solution.py:93
  170.8 0.0 copy-start.3
  170.8 1.6 broadcast_in_dim.67
  172.3 5.3 %all-to-all-start.2 = ((bf16[16,2,128,256]{3,2,1,0:T(8,128)(2,1)}), bf16[16,2,128,256]{3,2,1,0:T(8,128)(2,1)S(1)}, u32[]{:S(2)}, u32[]{:S(2)}) async-start(bf16[16,2,128,256]{3,2,1,0:T(8,128)(2,1)} %broadcast_in_dim.67), calls=%async_computation.2 | async-start | bytes 4194304 | tf_op jit(solution)/shard_map/all_to_all | solution.py:33
  177.6 0.2 reduce-scatter.2.cloned.1.call-start
  177.8 0.0 copy-done.3
  177.9 0.1 copy.37
  178.0 0.1 fusion.63
  178.1 0.2 broadcast_compare_fusion
  178.3 1.4 fusion.26
  179.8 1.9 copy.38
  181.6 0.1 slice_bitcast_fusion.6
  181.7 0.1 copy.53
  181.8 37.7 %all-to-all-done.2 = bf16[16,2,128,256]{3,2,1,0:T(8,128)(2,1)S(1)} async-done(((bf16[16,2,128,256]{3,2,1,0:T(8,128)(2,1)}), bf16[16,2,128,256]{3,2,1,0:T(8,128)(2,1)S(1)}, u32[]{:S(2)}, u32[]{:S(2)}) %all-to-all-start.2) | async-done | bytes 2097184 | tf_op jit(solution)/shard_map/all_to_all | solution.py:33
  219.5 0.1 copy.36
  219.7 2.7 fusion.2
  222.4 4.0 %fusion.3 = f32[2,8,128]{2,1,0:T(8,128)S(1)} fusion(f32[2,2048,128,8]{2,1,3,0:T(8,128)S(1)} %get-tuple-element.12, f32[2,8,128]{2,1,0:T(8,128)S(1)} %get-tuple-element.11, pred[2,128,2048]{1,2,0:T(8,128)(4,1)S(1)} %copy.38), kind=kLoop, calls=%fused_computation.5 | loop fusion | flops 20969472 | bytes 17317888 | tf_op jit(solution)/shard_map/reduce_sum | solution.py:123
  226.5 4.2 %divide_convert_fusion = bf16[2,128,1,8,128]{1,4,3,0,2:T(8,128)(2,1)S(1)} fusion(f32[2,2048,128,8]{2,1,3,0:T(8,128)S(1)} %get-tuple-element.12, f32[2,8,128]{2,1,0:T(8,128)S(1)} %get-tuple-element.11, pred[2,128,2048]{1,2,0:T(8,128)(4,1)S(1)} %copy.38, bf16[2,2048,256]{2,1,0:T(8,128)(2,1)S(1)} %bitcast.98, f32[2,128,8]{1,2,0:T(8,128)S(1)} %bitcast.106), kind=kOutput, calls=%fused_computation.42 | convolution fusion | flops 1095237632 | bytes 18890752 | tf_op jit(solution)/shard_map/skgqt,stkd->sqkgd/dot_general | solution.py:124
  230.7 63.3 %all-gather.5.cloned.1.call-done = bf16[8192,1024]{1,0:T(8,128)(2,1)} async-done(((bf16[512,1024]{1,0:T(8,128)(2,1)}), bf16[8192,1024]{1,0:T(8,128)(2,1)}) %all-gather.5.cloned.1.call-update) | async-done | bytes 16777232 | tf_op jit(solution)/shard_map/all_gather | solution.py:53
  294.0 9.7 %fusion.5 = bf16[2,128,8192]{2,1,0:T(8,128)(2,1)} fusion(bf16[2,128,1024]{1,2,0:T(8,128)(2,1)S(1)} %bitcast.109, bf16[8192,1024]{1,0:T(8,128)(2,1)} %all-gather.5.cloned.1.call-done), kind=kOutput, calls=%fused_computation.9 | convolution fusion | flops 4297064448 | bytes 21495808 | tf_op jit(solution)/shard_map/rk,nk->rn/dot_general | solution.py:135
  303.7 0.0 reduce-scatter.2.cloned.1.call-update
  303.7 0.7 copy-done.2
  304.4 3.4 fusion.80
  307.8 33.9 %reduce-scatter.2.cloned.1.call-done = bf16[2,128,1024]{2,1,0:T(8,128)(2,1)} async-done(((bf16[2,128,8192]{2,1,0:T(8,128)(2,1)}), bf16[2,128,1024]{2,1,0:T(8,128)(2,1)}) %reduce-scatter.2.cloned.1.call-update) | async-done | bytes 524304 | tf_op jit(solution)/shard_map/reduce_scatter | solution.py:138
  341.7 1.6 convolution_convert_fusion.1
  343.3 1.3 copy.44
  344.7 23.8 %all_to_all.20 = bf16[2,16,20,1024]{3,0,2,1:T(2,128)(2,1)S(1)} all-to-all(bf16[2,16,20,1024]{3,0,2,1:T(2,128)(2,1)S(1)} %bitcast.95), channel_id=1, replica_groups=mesh['seq'=8,'fsdp'=16] {'fsdp'}, dimensions={1} | all-to-all | bytes 2621440 | tf_op jit(solution)/shard_map/all_to_all | solution.py:154
  368.5 7.0 %convert_add_fusion = f32[2,1024,1024]{2,1,0:T(8,128)} fusion(bf16[2,1024,1024]{2,1,0:T(8,128)(2,1)} %param.10, s32[2,320]{1,0:T(2,128)S(1)} %get-tuple-element.10, bf16[2,320,1024]{2,0,1:T(2,128)(2,1)S(1)} %bitcast.100, s32[2,320]{1,0:T(2,128)S(1)} %get-tuple-element.9), kind=kOutput, calls=%fused_computation.14 | convolution fusion | flops 1767317504 | bytes 13898752 | tf_op jit(solution)/shard_map/skp,skc->spc/dot_general | solution.py:163
  (21 shorter events, 0.1 us)
Async XLA Ops:
  6.5 2.7 copy-start
  6.5 4.1 %copy-start.4 = (s32[2,16]{1,0:T(2,128)S(1)}, s32[2,16]{1,0:T(2,128)}, u32[]{:S(2)}) copy-start(s32[2,16]{1,0:T(2,128)} %param.12) | copy-start | bytes 388
  6.5 5.4 %copy-start.5 = (s32[2,320]{1,0:T(2,128)S(1)}, s32[2,320]{1,0:T(2,128)}, u32[]{:S(2)}) copy-start(s32[2,320]{1,0:T(2,128)} %param.11) | copy-start | bytes 7684
  6.5 152.1 %all-gather.3.cloned.1.call-start = ((), (), s32[]{:S(2)}) async-start(), calls=%async_computation.5 | async-start | bytes 22282240 | tf_op jit(solution)/shard_map/all_gather | solution.py:52
  9.2 284.8 %all-gather.5.cloned.1.call-start = ((), (), s32[]{:S(2)}) async-start(), calls=%async_computation.6 | async-start | bytes 17825792 | tf_op jit(solution)/shard_map/all_gather | solution.py:53
  18.5 42.1 %all-to-all-start = ((bf16[2,16,20,1024]{3,0,2,1:T(2,128)(2,1)}), bf16[2,16,20,1024]{3,0,2,1:T(2,128)(2,1)S(1)}, u32[]{:S(2)}, u32[]{:S(2)}) async-start(bf16[2,16,20,1024]{3,0,2,1:T(2,128)(2,1)} %bitcast), calls=%async_computation | async-start | bytes 2621440 | tf_op jit(solution)/shard_map/all_to_all | solution.py:68
  63.7 5.5 %copy-start.1 = (f32[8192]{0:T(1024)S(1)}, f32[8192]{0:T(1024)}, u32[]{:S(2)}) copy-start(f32[8192]{0:T(1024)} %param.15) | copy-start | bytes 98308
  63.7 55.2 %all-to-all-start.1 = ((bf16[8,256,1024]{2,1,0:T(8,128)(2,1)}), bf16[8,256,1024]{2,1,0:T(8,128)(2,1)}, u32[]{:S(2)}, u32[]{:S(2)}) async-start(bf16[8,256,1024]{2,1,0:T(8,128)(2,1)} %broadcast_in_dim.65), calls=%async_computation.1 | async-start | bytes 8388608 | tf_op jit(solution)/shard_map/all_to_all | solution.py:33
  170.8 7.1 %copy-start.3 = (s32[2,16,16]{2,1,0:T(8,128)S(1)}, s32[2,16,16]{2,1,0:T(8,128)}, u32[]{:S(2)}) copy-start(s32[2,16,16]{2,1,0:T(8,128)} %param.13) | copy-start | bytes 6148
  172.3 47.2 %all-to-all-start.2 = ((bf16[16,2,128,256]{3,2,1,0:T(8,128)(2,1)}), bf16[16,2,128,256]{3,2,1,0:T(8,128)(2,1)S(1)}, u32[]{:S(2)}, u32[]{:S(2)}) async-start(bf16[16,2,128,256]{3,2,1,0:T(8,128)(2,1)} %broadcast_in_dim.67), calls=%async_computation.2 | async-start | bytes 4194304 | tf_op jit(solution)/shard_map/all_to_all | solution.py:33
  177.6 164.1 %reduce-scatter.2.cloned.1.call-start = ((), (), s32[]{:S(2)}) async-start(), calls=%async_computation.7 | async-start | bytes 4718592 | tf_op jit(solution)/shard_map/reduce_scatter | solution.py:138
  303.7 0.7 copy-start.2
Sparse Core Ops, SparseCore 0:
  9.5 149.0 all-gather.2
  160.7 133.2 all-gather.4
  303.9 37.7 reduce-scatter.1

commit v7 on v3

--- a/solution.py
+++ b/solution.py
@@ -129,12 +129,11 @@
     partial_value = jnp.einsum(
         "rk,nk->rn", attended, w_out_t, preferred_element_type=jnp.float32
     )
-    summed = lax.psum_scatter(
-        partial_value.reshape(seq_count, own_rows, full_width).astype(jnp.bfloat16),
-        "seq",
-        scatter_dimension=2,
-        tiled=True,
-    ).astype(jnp.float32)
+    terms = lax.all_to_all(
+        partial_value.astype(jnp.bfloat16).reshape(row_total, seq_size, part_width),
+        "seq", split_axis=1, concat_axis=1, tiled=True,
+    )
+    summed = jnp.sum(terms.astype(jnp.float32), axis=1).reshape(seq_count, own_rows, part_width)
     update = (gate_value.reshape(seq_count, own_rows, 1) * summed).astype(jnp.bfloat16)
 
     first_back = jnp.mod(owner_idx - starts, fsdp_size)[:, :, None]

time: 382 us -> 414 us (1.084)
  waiting for transfers between devices: 201 us -> 223 us
  starting transfers between devices: 12.7 us -> 17.4 us
    all_to_all x0 -> x1, waiting for transfers between devices: none -> 46 us  [shards(): lax.all_to_all(partial_value.astype(jnp.bfloat16).reshape(row_total, seq_...]
    reduce_scatter x1 -> x0, waiting for transfers between devices: 33.9 us -> none  [shards(): lax.psum_scatter(partial_value.reshape(seq_count, own_rows, full_width).a...]
    all_gather x1, waiting for transfers between devices: 62.5 us -> 72.7 us  [shards(): w_out_t = lax.all_gather(w_out.T, 'fsdp', axis=0, tiled=True)]
    all_to_all x0 -> x1, starting transfers between devices: none -> 4.94 us  [shards(): lax.all_to_all(partial_value.astype(jnp.bfloat16).reshape(row_total, seq_...]
    unnamed x17 -> x14, local copies, waits for them, and re-layouts: 8.54 us -> 6.54 us
  transfers between devices with their start and end apart: 5 -> 5, of which waited for: 5 -> 5; matrix products, arithmetic and copies ran while one was open for 14% -> 13% of each run, Pallas kernels for 0% -> 0%
where the time goes in v7:
time: 414 us; the launch traced here: 413 us
  waiting for transfers between devices  223 us (54%)
  blocking collectives  79.3 us (19%)
  matrix products  47.9 us (12%)
  local copies, waits for them, and re-layouts  20.6 us (5%)
  starting transfers between devices  17.4 us (4%)
  between operations  13.7 us (3%)
  other arithmetic  11.8 us (3%)
    all_gather x1, waiting for transfers between devices, shards(): w_out_t = lax.all_gather(w_out.T, 'fsdp', axis=0, tiled=True)  72.7 us
    all_to_all x1, blocking collectives, gather_all(): lax.all_to_all(copies, axis_name, split_axis=0, concat_axis=0, tiled=True)  54.8 us
    all_to_all x1, waiting for transfers between devices, shards(): lax.all_to_all(partial_value.astype(jnp.bfloat16).reshape(row_total, seq_...  46 us
    all_to_all x1, waiting for transfers between devices, gather_all(): lax.all_to_all(copies, axis_name, split_axis=0, concat_axis=0, tiled=True)  35.3 us
    all_to_all x1, waiting for transfers between devices, shards(): lax.all_to_all(send_rows, 'fsdp', split_axis=1, concat_axis=1, tiled=True)  34.7 us
    all_gather x1, waiting for transfers between devices, shards(): w_qkv = lax.all_gather(packed, 'fsdp', axis=0, tiled=True)  33.2 us
    all_to_all x1, blocking collectives, shards(): lax.all_to_all(back_rows, 'fsdp', split_axis=1, concat_axis=1, tiled=True)  24.5 us
    dot_general x1, matrix products, shards(): jnp.dot(normed, w_qkv, preferred_element_type=jnp.float32)  13.6 us
  transfers between devices with their start and end apart: 5, of which 5 were waited for; matrix products, arithmetic and copies ran while one was open for 13% of the time, Pallas kernels for 0%

profile of v7, /device:TPU:0, one launch (start us, length us, event | category | flops | bytes accessed | tf_op | source)
XLA Modules:
  0.0 413.3 jit_solution(5676137011244387645)
XLA Ops:
  6.5 0.0 all-gather.3.cloned.1.call-start
  6.5 2.6 pad_maximum_fusion
  9.1 0.0 all-gather.3.cloned.1.call-update
  9.1 0.0 all-gather.5.cloned.1.call-start
  9.2 0.7 all-gather.5.cloned.1.call-update
  9.9 0.0 copy-done.2
  9.9 0.2 reduce_window_sum.11
  10.1 0.2 dynamic-slice_reduce_fusion
  10.3 0.1 and_select_fusion.3
  10.4 0.1 add.256
  10.5 0.1 add.257
  10.6 0.1 add.246
  10.7 0.1 add.249
  10.7 0.1 add.250
  10.8 0.1 add.243
  10.9 0.1 add.244
  11.0 0.1 lt.92
  11.1 0.1 lt.93
  11.2 0.0 copy-done.3
  11.2 0.3 select_reduce_fusion
  11.5 0.1 compare_select_fusion.3
  11.6 3.8 fusion.13
  15.3 2.4 copy.36
  17.7 7.1 %all-to-all-start = ((bf16[2,16,20,1024]{3,0,2,1:T(2,128)(2,1)}), bf16[2,16,20,1024]{3,0,2,1:T(2,128)(2,1)S(1)}, u32[]{:S(2)}, u32[]{:S(2)}) async-start(bf16[2,16,20,1024]{3,0,2,1:T(2,128)(2,1)} %bitcast), calls=%async_computation | async-start | bytes 2621440 | tf_op jit(solution)/shard_map/all_to_all | solution.py:68
  24.9 0.1 convert_reduce_fusion.1
  25.0 0.1 select_reduce_fusion.1
  25.1 34.7 %all-to-all-done = bf16[2,16,20,1024]{3,0,2,1:T(2,128)(2,1)S(1)} async-done(((bf16[2,16,20,1024]{3,0,2,1:T(2,128)(2,1)}), bf16[2,16,20,1024]{3,0,2,1:T(2,128)(2,1)S(1)}, u32[]{:S(2)}, u32[]{:S(2)}) %all-to-all-start) | async-done | bytes 1310752 | tf_op jit(solution)/shard_map/all_to_all | solution.py:68
  59.8 0.6 fusion.22
  60.4 0.5 broadcast_in_dim.62
  61.0 54.8 %all_to_all.25 = bf16[8,2,128,1024]{3,2,1,0:T(8,128)(2,1)S(1)} all-to-all(bf16[8,2,128,1024]{3,2,1,0:T(8,128)(2,1)S(1)} %broadcast_in_dim.62), channel_id=1, replica_groups=mesh['seq'=8,'fsdp'=16] {'seq'}, dimensions={0} | all-to-all | bytes 8388608 | tf_op jit(solution)/shard_map/all_to_all | solution.py:33
  115.8 2.3 copy.38
  118.1 6.3 %copy.55 = bf16[32,8,8,1024]{3,1,2,0:T(8,128)(2,1)} copy(bf16[32,8,8,1024]{3,2,1,0:T(8,128)(2,1)S(1)} %bitcast.104) | data formatting | bytes 8388608
  124.5 0.9 multiply_reduce_fusion
  125.4 33.2 %all-gather.3.cloned.1.call-done = bf16[8192,1280]{1,0:T(8,128)(2,1)} async-done(((bf16[512,1280]{1,0:T(8,128)(2,1)}), bf16[8192,1280]{1,0:T(8,128)(2,1)}) %all-gather.3.cloned.1.call-update) | async-done | bytes 20971536 | tf_op jit(solution)/shard_map/all_gather | solution.py:52
  158.6 0.0 copy-done.4
  158.6 13.6 %fusion.11 = bf16[256,1280]{1,0:T(8,128)(2,1)S(1)} fusion(bf16[8192,1280]{1,0:T(8,128)(2,1)} %all-gather.3.cloned.1.call-done, bf16[256,8192]{1,0:T(8,128)(2,1)} %bitcast.101, f32[8192]{0:T(1024)S(1)} %copy-done.4, f32[256]{0:T(256)S(1)} %rsqrt_bitcast_fusion), kind=kOutput, calls=%fused_computation.20 | convolution fusion | flops 5377425408 | bytes 25854976 | tf_op jit(solution)/shard_map/dot_general | solution.py:90
  172.2 0.0 copy-start.1
  172.3 1.6 broadcast_in_dim.64
  173.8 5.3 %all-to-all-start.2 = ((bf16[16,2,128,256]{3,2,1,0:T(8,128)(2,1)}), bf16[16,2,128,256]{3,2,1,0:T(8,128)(2,1)S(1)}, u32[]{:S(2)}, u32[]{:S(2)}) async-start(bf16[16,2,128,256]{3,2,1,0:T(8,128)(2,1)} %broadcast_in_dim.64), calls=%async_computation.2 | async-start | bytes 4194304 | tf_op jit(solution)/shard_map/all_to_all | solution.py:33
  179.1 0.0 copy-done.1
  179.1 0.1 copy.40
  179.3 0.1 fusion.51
  179.4 0.2 broadcast_compare_fusion
  179.6 1.4 fusion.12
  181.0 1.9 copy.41
  182.9 0.1 slice_bitcast_fusion.6
  183.0 0.1 copy.56
  183.1 35.3 %all-to-all-done.2 = bf16[16,2,128,256]{3,2,1,0:T(8,128)(2,1)S(1)} async-done(((bf16[16,2,128,256]{3,2,1,0:T(8,128)(2,1)}), bf16[16,2,128,256]{3,2,1,0:T(8,128)(2,1)S(1)}, u32[]{:S(2)}, u32[]{:S(2)}) %all-to-all-start.2) | async-done | bytes 2097184 | tf_op jit(solution)/shard_map/all_to_all | solution.py:33
  218.4 0.2 copy.39
  218.6 2.7 fusion
  221.3 4.0 fusion.1
  225.4 4.2 %divide_convert_fusion = bf16[2,128,1,8,128]{1,4,3,0,2:T(8,128)(2,1)S(1)} fusion(f32[2,2048,128,8]{2,1,3,0:T(8,128)S(1)} %get-tuple-element.12, f32[2,8,128]{2,1,0:T(8,128)S(1)} %get-tuple-element.11, pred[2,128,2048]{1,2,0:T(8,128)(4,1)S(1)} %copy.41, bf16[2,2048,256]{2,1,0:T(8,128)(2,1)S(1)} %bitcast.110, f32[2,128,8]{1,2,0:T(8,128)S(1)} %bitcast.119), kind=kOutput, calls=%fused_computation.38 | convolution fusion | flops 1095237632 | bytes 18890752 | tf_op jit(solution)/shard_map/skgqt,stkd->sqkgd/dot_general | solution.py:118
  229.6 0.3 copy.45
  229.9 72.7 %all-gather.5.cloned.1.call-done = bf16[8192,1024]{0,1:T(8,128)(2,1)} async-done(((bf16[512,1024]{0,1:T(8,128)(2,1)}), bf16[8192,1024]{0,1:T(8,128)(2,1)}) %all-gather.5.cloned.1.call-update) | async-done | bytes 16777232 | tf_op jit(solution)/shard_map/all_gather | solution.py:53
  302.6 10.5 %convolution_convert_fusion = bf16[256,8192]{1,0:T(8,128)(2,1)S(1)} fusion(bf16[8192,1024]{0,1:T(8,128)(2,1)} %all-gather.5.cloned.1.call-done, bf16[32,8,8,128]{3,2,1,0:T(8,128)(2,1)S(1)} %bitcast.116), kind=kOutput, calls=%fused_computation.5 | convolution fusion | flops 4297064448 | bytes 21495808 | tf_op jit(solution)/shard_map/rk,nk->rn/dot_general | solution.py:129
  313.1 2.5 copy.75
  315.6 4.9 %all-to-all-start.3 = ((bf16[256,8,1024]{2,0,1:T(8,128)(2,1)}), bf16[256,8,1024]{2,0,1:T(8,128)(2,1)}, u32[]{:S(2)}, u32[]{:S(2)}) async-start(bf16[256,8,1024]{2,0,1:T(8,128)(2,1)} %bitcast.103), calls=%async_computation.3 | async-start | bytes 8388608 | tf_op jit(solution)/shard_map/all_to_all | solution.py:132
  320.6 3.4 fusion.68
  323.9 46.0 %all-to-all-done.3 = bf16[256,8,1024]{2,0,1:T(8,128)(2,1)} async-done(((bf16[256,8,1024]{2,0,1:T(8,128)(2,1)}), bf16[256,8,1024]{2,0,1:T(8,128)(2,1)}, u32[]{:S(2)}, u32[]{:S(2)}) %all-to-all-start.3) | async-done | bytes 4194336 | tf_op jit(solution)/shard_map/all_to_all | solution.py:132
  369.9 3.2 convert_reduce_fusion
  373.1 0.6 convolution_convert_fusion.2
  373.6 1.3 copy.47
  375.0 24.5 %all_to_all.26 = bf16[2,16,20,1024]{3,0,2,1:T(2,128)(2,1)S(1)} all-to-all(bf16[2,16,20,1024]{3,0,2,1:T(2,128)(2,1)S(1)} %bitcast.106), channel_id=1, replica_groups=mesh['seq'=8,'fsdp'=16] {'fsdp'}, dimensions={1} | all-to-all | bytes 2621440 | tf_op jit(solution)/shard_map/all_to_all | solution.py:147
  399.4 7.0 %convert_add_fusion = f32[2,1024,1024]{2,1,0:T(8,128)} fusion(bf16[2,1024,1024]{2,1,0:T(8,128)(2,1)} %param.10, s32[2,320]{1,0:T(2,128)S(1)} %get-tuple-element.10, bf16[2,320,1024]{2,0,1:T(2,128)(2,1)S(1)} %bitcast.112, s32[2,320]{1,0:T(2,128)S(1)} %get-tuple-element.9), kind=kOutput, calls=%fused_computation.10 | convolution fusion | flops 1767317504 | bytes 13898752 | tf_op jit(solution)/shard_map/skp,skc->spc/dot_general | solution.py:156
  (20 shorter events, 0.1 us)
Async XLA Ops:
  6.5 3.3 copy-start.2
  6.5 4.7 %copy-start.3 = (s32[2,320]{1,0:T(2,128)S(1)}, s32[2,320]{1,0:T(2,128)}, u32[]{:S(2)}) copy-start(s32[2,320]{1,0:T(2,128)} %param.11) | copy-start | bytes 7684
  6.5 152.1 %all-gather.3.cloned.1.call-start = ((), (), s32[]{:S(2)}) async-start(), calls=%async_computation.5 | async-start | bytes 22282240 | tf_op jit(solution)/shard_map/all_gather | solution.py:52
  9.1 293.5 %all-gather.5.cloned.1.call-start = ((), (), s32[]{:S(2)}) async-start(), calls=%async_computation.6 | async-start | bytes 17825792 | tf_op jit(solution)/shard_map/all_gather | solution.py:53
  17.7 42.1 %all-to-all-start = ((bf16[2,16,20,1024]{3,0,2,1:T(2,128)(2,1)}), bf16[2,16,20,1024]{3,0,2,1:T(2,128)(2,1)S(1)}, u32[]{:S(2)}, u32[]{:S(2)}) async-start(bf16[2,16,20,1024]{3,0,2,1:T(2,128)(2,1)} %bitcast), calls=%async_computation | async-start | bytes 2621440 | tf_op jit(solution)/shard_map/all_to_all | solution.py:68
  124.5 34.1 %copy-start.4 = (f32[8192]{0:T(1024)S(1)}, f32[8192]{0:T(1024)}, u32[]{:S(2)}) copy-start(f32[8192]{0:T(1024)} %param.15) | copy-start | bytes 98308
  172.2 6.9 %copy-start.1 = (s32[2,16,16]{2,1,0:T(8,128)S(1)}, s32[2,16,16]{2,1,0:T(8,128)}, u32[]{:S(2)}) copy-start(s32[2,16,16]{2,1,0:T(8,128)} %param.13) | copy-start | bytes 6148
  173.8 44.6 %all-to-all-start.2 = ((bf16[16,2,128,256]{3,2,1,0:T(8,128)(2,1)}), bf16[16,2,128,256]{3,2,1,0:T(8,128)(2,1)S(1)}, u32[]{:S(2)}, u32[]{:S(2)}) async-start(bf16[16,2,128,256]{3,2,1,0:T(8,128)(2,1)} %broadcast_in_dim.64), calls=%async_computation.2 | async-start | bytes 4194304 | tf_op jit(solution)/shard_map/all_to_all | solution.py:33
  315.6 4.9 %copy-start = (bf16[8192]{0:T(1024)(128)(2,1)S(1)}, bf16[8192]{0:T(1024)(128)(2,1)}, u32[]{:S(2)}) copy-start(bf16[8192]{0:T(1024)(128)(2,1)} %param.14) | copy-start | bytes 49156
  315.6 54.3 %all-to-all-start.3 = ((bf16[256,8,1024]{2,0,1:T(8,128)(2,1)}), bf16[256,8,1024]{2,0,1:T(8,128)(2,1)}, u32[]{:S(2)}, u32[]{:S(2)}) async-start(bf16[256,8,1024]{2,0,1:T(8,128)(2,1)} %bitcast.103), calls=%async_computation.3 | async-start | bytes 8388608 | tf_op jit(solution)/shard_map/all_to_all | solution.py:132
Sparse Core Ops, SparseCore 0:
  9.5 149.0 all-gather.2
  160.7 141.8 all-gather.4

commit v8 on v3

--- a/solution.py
+++ b/solution.py
@@ -48,9 +48,12 @@
     in_rows, q_cols = w_query.shape
     kv_cols = w_key.shape[1]
     qkv_cols = q_cols + 2 * kv_cols
-    packed = jnp.concatenate([w_query, w_key, w_value], axis=1)
-    w_qkv = lax.all_gather(packed, "fsdp", axis=0, tiled=True)
-    w_out_t = lax.all_gather(w_out.T, "fsdp", axis=0, tiled=True)
+    early_k = w_out.shape[0] // 2
+    packed = jnp.concatenate([w_query, w_key, w_value, w_out[:early_k].T], axis=1)
+    first = lax.all_gather(packed, "fsdp", axis=0, tiled=True)
+    w_qkv = first[:, :qkv_cols]
+    w_out_early = first[:, qkv_cols:]
+    w_out_late = lax.all_gather(w_out[early_k:].T, "fsdp", axis=0, tiled=True)
 
     starts = jnp.cumsum(keep_count, axis=1) - keep_count
     range_ends = starts + keep_count
@@ -127,7 +130,9 @@
         .reshape(row_total, local_heads * HD)
     )
     partial_value = jnp.einsum(
-        "rk,nk->rn", attended, w_out_t, preferred_element_type=jnp.float32
+        "rk,nk->rn", attended[:, :early_k], w_out_early, preferred_element_type=jnp.float32
+    ) + jnp.einsum(
+        "rk,nk->rn", attended[:, early_k:], w_out_late, preferred_element_type=jnp.float32
     )
     summed = lax.psum_scatter(
         partial_value.reshape(seq_count, own_rows, full_width).astype(jnp.bfloat16),

time: 382 us -> 392 us (1.026)
  matrix products: 48.2 us -> 57.9 us
    dot_general x1 -> x2, matrix products: 9.74 us -> 19.3 us  [the longest x1 10.1 us: shards(): jnp.einsum('rk,nk->rn', attended[:, early_k:], w_out_late, preferred_elem...]
    all_to_all x1, waiting for transfers between devices: 37 us -> 31.4 us  [gather_all(): lax.all_to_all(copies, axis_name, split_axis=0, concat_axis=0, tiled=True)]
    unnamed x17 -> x15, local copies, waits for them, and re-layouts: 8.54 us -> 7.25 us
  transfers between devices with their start and end apart: 5 -> 5, of which waited for: 5 -> 5; matrix products, arithmetic and copies ran while one was open for 14% -> 16% of each run, Pallas kernels for 0% -> 0%
where the time goes in v8:
time: 392 us; the launch traced here: 391 us
  waiting for transfers between devices  199 us (51%)
  blocking collectives  78.6 us (20%)
  matrix products  57.9 us (15%)
  local copies, waits for them, and re-layouts  21.2 us (5%)
  between operations  13.4 us (3%)
  starting transfers between devices  12.5 us (3%)
  other arithmetic  8.83 us (2%)
    all_gather x1, waiting for transfers between devices, shards(): first = lax.all_gather(packed, 'fsdp', axis=0, tiled=True)  75.9 us
    all_to_all x1, blocking collectives, gather_all(): lax.all_to_all(copies, axis_name, split_axis=0, concat_axis=0, tiled=True)  54.8 us
    all_to_all x1, waiting for transfers between devices, shards(): lax.all_to_all(send_rows, 'fsdp', split_axis=1, concat_axis=1, tiled=True)  34.7 us
    reduce_scatter x1, waiting for transfers between devices, shards(): lax.psum_scatter(partial_value.reshape(seq_count, own_rows, full_width).a...  33.7 us
    all_to_all x1, waiting for transfers between devices, gather_all(): lax.all_to_all(copies, axis_name, split_axis=0, concat_axis=0, tiled=True)  31.4 us
    all_to_all x1, blocking collectives, shards(): lax.all_to_all(back_rows, 'fsdp', split_axis=1, concat_axis=1, tiled=True)  23.7 us
    all_gather x1, waiting for transfers between devices, shards(): w_out_late = lax.all_gather(w_out[early_k:].T, 'fsdp', axis=0, tiled=True)  22.5 us
    dot_general x1, matrix products, shards(): jnp.dot(normed, w_qkv, preferred_element_type=jnp.float32)  13.9 us
  transfers between devices with their start and end apart: 5, of which 5 were waited for; matrix products, arithmetic and copies ran while one was open for 16% of the time, Pallas kernels for 0%

profile of v8, /device:TPU:0, one launch (start us, length us, event | category | flops | bytes accessed | tf_op | source)
XLA Modules:
  0.0 391.4 jit_solution(12874991058570906386)
XLA Ops:
  6.5 0.0 all-gather.3.cloned.1.call-start
  6.5 2.1 slice_bitcast_fusion.7
  8.6 0.2 copy.41
  8.9 2.7 pad_maximum_fusion
  11.6 0.0 all-gather.3.cloned.1.call-update
  11.6 0.0 all-gather.5.cloned.1.call-start
  11.7 0.7 all-gather.5.cloned.1.call-update
  12.4 0.2 reduce_window_sum.11
  12.6 0.2 dynamic-slice_reduce_fusion
  12.8 0.1 and_select_fusion.3
  12.9 0.1 add.261
  13.0 0.1 add.262
  13.1 0.1 add.251
  13.2 0.1 add.254
  13.2 0.1 add.255
  13.3 0.1 add.248
  13.4 0.1 add.249
  13.5 0.1 lt.92
  13.6 0.1 lt.93
  13.7 0.3 select_reduce_fusion
  14.0 0.1 compare_select_fusion.3
  14.1 3.8 fusion.19
  17.8 2.4 copy.38
  20.3 7.1 %all-to-all-start = ((bf16[2,16,20,1024]{3,0,2,1:T(2,128)(2,1)}), bf16[2,16,20,1024]{3,0,2,1:T(2,128)(2,1)S(1)}, u32[]{:S(2)}, u32[]{:S(2)}) async-start(bf16[2,16,20,1024]{3,0,2,1:T(2,128)(2,1)} %bitcast), calls=%async_computation | async-start | bytes 2621440 | tf_op jit(solution)/shard_map/all_to_all | solution.py:71
  27.4 0.1 convert_reduce_fusion
  27.5 0.1 select_reduce_fusion.1
  27.6 34.7 %all-to-all-done = bf16[2,16,20,1024]{3,0,2,1:T(2,128)(2,1)S(1)} async-done(((bf16[2,16,20,1024]{3,0,2,1:T(2,128)(2,1)}), bf16[2,16,20,1024]{3,0,2,1:T(2,128)(2,1)S(1)}, u32[]{:S(2)}, u32[]{:S(2)}) %all-to-all-start) | async-done | bytes 1310752 | tf_op jit(solution)/shard_map/all_to_all | solution.py:71
  62.3 0.6 fusion.28
  62.9 0.5 broadcast_in_dim.62
  63.5 54.8 %all_to_all.20 = bf16[8,2,128,1024]{3,2,1,0:T(8,128)(2,1)S(1)} all-to-all(bf16[8,2,128,1024]{3,2,1,0:T(8,128)(2,1)S(1)} %broadcast_in_dim.62), channel_id=1, replica_groups=mesh['seq'=8,'fsdp'=16] {'seq'}, dimensions={0} | all-to-all | bytes 8388608 | tf_op jit(solution)/shard_map/all_to_all | solution.py:33
  118.3 2.3 copy.40
  120.6 6.3 %copy.56 = bf16[32,8,8,1024]{3,1,2,0:T(8,128)(2,1)} copy(bf16[32,8,8,1024]{3,2,1,0:T(8,128)(2,1)S(1)} %bitcast.101) | data formatting | bytes 8388608
  126.9 0.9 multiply_reduce_fusion
  127.8 75.9 %all-gather.3.cloned.1.call-done = bf16[8192,1792]{1,0:T(8,128)(2,1)} async-done(((bf16[512,1792]{1,0:T(8,128)(2,1)}), bf16[8192,1792]{1,0:T(8,128)(2,1)}) %all-gather.3.cloned.1.call-update) | async-done | bytes 29360144 | tf_op jit(solution)/shard_map/all_gather | solution.py:53
  203.7 13.9 %fusion.15 = bf16[256,1280]{1,0:T(8,128)(2,1)S(1)} fusion(bf16[8192,1792]{1,0:T(8,128)(2,1)} %all-gather.3.cloned.1.call-done, bf16[256,8192]{1,0:T(8,128)(2,1)} %bitcast.99, f32[8192]{0:T(1024)S(1)} %copy-done.4, f32[256]{0:T(256)S(1)} %rsqrt_bitcast_fusion), kind=kOutput, calls=%fused_computation.22 | convolution fusion | flops 5377425408 | bytes 25854976 | tf_op jit(solution)/shard_map/dot_general | solution.py:93
  217.6 0.0 copy-start.1
  217.6 1.6 broadcast_in_dim.64
  219.2 5.3 %all-to-all-start.2 = ((bf16[16,2,128,256]{3,2,1,0:T(8,128)(2,1)}), bf16[16,2,128,256]{3,2,1,0:T(8,128)(2,1)S(1)}, u32[]{:S(2)}, u32[]{:S(2)}) async-start(bf16[16,2,128,256]{3,2,1,0:T(8,128)(2,1)} %broadcast_in_dim.64), calls=%async_computation.2 | async-start | bytes 4194304 | tf_op jit(solution)/shard_map/all_to_all | solution.py:33
  224.4 0.0 reduce-scatter.2.cloned.1.call-start
  224.5 0.1 copy.43
  224.7 0.1 fusion.57
  224.8 0.2 broadcast_compare_fusion
  225.0 1.4 fusion.18
  226.4 1.9 copy.44
  228.3 0.1 slice_bitcast_fusion.6
  228.3 0.1 copy.57
  228.4 31.4 %all-to-all-done.2 = bf16[16,2,128,256]{3,2,1,0:T(8,128)(2,1)S(1)} async-done(((bf16[16,2,128,256]{3,2,1,0:T(8,128)(2,1)}), bf16[16,2,128,256]{3,2,1,0:T(8,128)(2,1)S(1)}, u32[]{:S(2)}, u32[]{:S(2)}) %all-to-all-start.2) | async-done | bytes 2097184 | tf_op jit(solution)/shard_map/all_to_all | solution.py:33
  259.9 0.2 copy.42
  260.1 2.7 fusion.2
  262.8 4.1 %fusion.3 = f32[2,8,128]{2,1,0:T(8,128)S(1)} fusion(f32[2,2048,128,8]{2,1,3,0:T(8,128)S(1)} %get-tuple-element.14, f32[2,8,128]{2,1,0:T(8,128)S(1)} %get-tuple-element.13, pred[2,128,2048]{1,2,0:T(8,128)(4,1)S(1)} %copy.44), kind=kLoop, calls=%fused_computation.5 | loop fusion | flops 20969472 | bytes 17317888 | tf_op jit(solution)/shard_map/reduce_sum | solution.py:120
  266.9 4.2 %divide_convert_fusion = bf16[2,128,1,8,128]{1,4,3,0,2:T(8,128)(2,1)S(1)} fusion(f32[2,2048,128,8]{2,1,3,0:T(8,128)S(1)} %get-tuple-element.14, f32[2,8,128]{2,1,0:T(8,128)S(1)} %get-tuple-element.13, pred[2,128,2048]{1,2,0:T(8,128)(4,1)S(1)} %copy.44, bf16[2,2048,256]{2,1,0:T(8,128)(2,1)S(1)} %bitcast.108, f32[2,128,8]{1,2,0:T(8,128)S(1)} %bitcast.116), kind=kOutput, calls=%fused_computation.40 | convolution fusion | flops 1095237632 | bytes 18890752 | tf_op jit(solution)/shard_map/skgqt,stkd->sqkgd/dot_general | solution.py:121
  271.1 0.3 copy.48
  271.4 0.1 copy.72
  271.5 9.2 %fusion.7 = f32[256,8192]{1,0:T(8,128)} fusion(bf16[8192,1792]{1,0:T(8,128)(2,1)} %all-gather.3.cloned.1.call-done, bf16[256,1024]{1,0:T(8,128)(2,1)S(1)} %bitcast.105), kind=kOutput, calls=%fused_computation.10 | convolution fusion | flops 2147483648 | bytes 17039360 | tf_op jit(solution)/shard_map/rk,nk->rn/dot_general | solution.py:132
  280.7 22.5 %all-gather.5.cloned.1.call-done = bf16[8192,512]{0,1:T(8,128)(2,1)} async-done(((bf16[512,512]{0,1:T(8,128)(2,1)}), bf16[8192,512]{0,1:T(8,128)(2,1)}) %all-gather.5.cloned.1.call-update) | async-done | bytes 8388624 | tf_op jit(solution)/shard_map/all_gather | solution.py:56
  303.2 10.1 %fusion.5 = bf16[256,8192]{1,0:T(8,128)(2,1)} fusion(f32[256,8192]{1,0:T(8,128)} %fusion.7, bf16[8192,512]{0,1:T(8,128)(2,1)} %all-gather.5.cloned.1.call-done, bf16[256,1024]{1,0:T(8,128)(2,1)S(1)} %bitcast.106), kind=kOutput, calls=%fused_computation.8 | convolution fusion | flops 2151677952 | bytes 21233664 | tf_op jit(solution)/shard_map/rk,nk->rn/dot_general | solution.py:134
  313.3 0.0 reduce-scatter.2.cloned.1.call-update
  313.3 0.7 copy-done
  314.1 3.4 fusion.74
  317.4 33.7 %reduce-scatter.2.cloned.1.call-done = bf16[2,128,1024]{2,1,0:T(8,128)(2,1)} async-done(((bf16[2,128,8192]{2,1,0:T(8,128)(2,1)}), bf16[2,128,1024]{2,1,0:T(8,128)(2,1)}) %reduce-scatter.2.cloned.1.call-update) | async-done | bytes 524304 | tf_op jit(solution)/shard_map/reduce_scatter | solution.py:137
  351.1 1.6 convolution_convert_fusion.1
  352.7 1.3 copy.49
  354.1 23.7 %all_to_all.21 = bf16[2,16,20,1024]{3,0,2,1:T(2,128)(2,1)S(1)} all-to-all(bf16[2,16,20,1024]{3,0,2,1:T(2,128)(2,1)S(1)} %bitcast.104), channel_id=1, replica_groups=mesh['seq'=8,'fsdp'=16] {'fsdp'}, dimensions={1} | all-to-all | bytes 2621440 | tf_op jit(solution)/shard_map/all_to_all | solution.py:153
  377.8 7.0 %convert_add_fusion = f32[2,1024,1024]{2,1,0:T(8,128)} fusion(bf16[2,1024,1024]{2,1,0:T(8,128)(2,1)} %param.10, s32[2,320]{1,0:T(2,128)S(1)} %get-tuple-element.12, bf16[2,320,1024]{2,0,1:T(2,128)(2,1)S(1)} %bitcast.111, s32[2,320]{1,0:T(2,128)S(1)} %get-tuple-element.11), kind=kOutput, calls=%fused_computation.14 | convolution fusion | flops 1767317504 | bytes 13898752 | tf_op jit(solution)/shard_map/skp,skc->spc/dot_general | solution.py:162
  (23 shorter events, 0.1 us)
Async XLA Ops:
  6.5 5.9 %copy-start.2 = (s32[2,16]{1,0:T(2,128)S(1)}, s32[2,16]{1,0:T(2,128)}, u32[]{:S(2)}) copy-start(s32[2,16]{1,0:T(2,128)} %param.12) | copy-start | bytes 388
  6.5 7.2 %copy-start.3 = (s32[2,320]{1,0:T(2,128)S(1)}, s32[2,320]{1,0:T(2,128)}, u32[]{:S(2)}) copy-start(s32[2,320]{1,0:T(2,128)} %param.11) | copy-start | bytes 7684
  6.5 197.2 %all-gather.3.cloned.1.call-start = ((), (), s32[]{:S(2)}) async-start(), calls=%async_computation.5 | async-start | bytes 31195136 | tf_op jit(solution)/shard_map/all_gather | solution.py:53
  11.6 291.6 %all-gather.5.cloned.1.call-start = ((), (), s32[]{:S(2)}) async-start(), calls=%async_computation.6 | async-start | bytes 8912896 | tf_op jit(solution)/shard_map/all_gather | solution.py:56
  20.3 42.1 %all-to-all-start = ((bf16[2,16,20,1024]{3,0,2,1:T(2,128)(2,1)}), bf16[2,16,20,1024]{3,0,2,1:T(2,128)(2,1)S(1)}, u32[]{:S(2)}, u32[]{:S(2)}) async-start(bf16[2,16,20,1024]{3,0,2,1:T(2,128)(2,1)} %bitcast), calls=%async_computation | async-start | bytes 2621440 | tf_op jit(solution)/shard_map/all_to_all | solution.py:71
  126.9 76.8 %copy-start.4 = (f32[8192]{0:T(1024)S(1)}, f32[8192]{0:T(1024)}, u32[]{:S(2)}) copy-start(f32[8192]{0:T(1024)} %param.15) | copy-start | bytes 98308
  217.6 6.9 %copy-start.1 = (s32[2,16,16]{2,1,0:T(8,128)S(1)}, s32[2,16,16]{2,1,0:T(8,128)}, u32[]{:S(2)}) copy-start(s32[2,16,16]{2,1,0:T(8,128)} %param.13) | copy-start | bytes 6148
  219.2 40.7 %all-to-all-start.2 = ((bf16[16,2,128,256]{3,2,1,0:T(8,128)(2,1)}), bf16[16,2,128,256]{3,2,1,0:T(8,128)(2,1)S(1)}, u32[]{:S(2)}, u32[]{:S(2)}) async-start(bf16[16,2,128,256]{3,2,1,0:T(8,128)(2,1)} %broadcast_in_dim.64), calls=%async_computation.2 | async-start | bytes 4194304 | tf_op jit(solution)/shard_map/all_to_all | solution.py:33
  224.4 126.7 %reduce-scatter.2.cloned.1.call-start = ((), (), s32[]{:S(2)}) async-start(), calls=%async_computation.7 | async-start | bytes 4718592 | tf_op jit(solution)/shard_map/reduce_scatter | solution.py:137
  313.3 0.7 copy-start
Sparse Core Ops, SparseCore 0:
  11.7 191.9 all-gather.2
  205.8 97.3 all-gather.4
  313.5 37.5 reduce-scatter.1

commit v9 on v3

--- a/solution.py
+++ b/solution.py
@@ -48,7 +48,10 @@
     in_rows, q_cols = w_query.shape
     kv_cols = w_key.shape[1]
     qkv_cols = q_cols + 2 * kv_cols
-    packed = jnp.concatenate([w_query, w_key, w_value], axis=1)
+    packed = jnp.zeros((in_rows, qkv_cols), w_query.dtype)
+    packed = lax.dynamic_update_slice(packed, w_query, (0, 0))
+    packed = lax.dynamic_update_slice(packed, w_key, (0, q_cols))
+    packed = lax.dynamic_update_slice(packed, w_value, (0, q_cols + kv_cols))
     w_qkv = lax.all_gather(packed, "fsdp", axis=0, tiled=True)
     w_out_t = lax.all_gather(w_out.T, "fsdp", axis=0, tiled=True)
 

time: 382 us -> 384 us (level)
  local copies, waits for them, and re-layouts: 19.8 us -> 24.1 us
    unnamed x17 -> x19, local copies, waits for them, and re-layouts: 8.54 us -> 9.6 us
where the time goes in v9:
time: 384 us
  waiting for transfers between devices  200 us (52%)
  blocking collectives  78.7 us (20%)
  matrix products  48.1 us (13%)
  local copies, waits for them, and re-layouts  24.1 us (6%)
  between operations  13.4 us (3%)
  starting transfers between devices  12.7 us (3%)
  other arithmetic  6.09 us (2%)
    all_gather x1, waiting for transfers between devices, shards(): w_out_t = lax.all_gather(w_out.T, 'fsdp', axis=0, tiled=True)  62.5 us
    all_to_all x1, blocking collectives, gather_all(): lax.all_to_all(copies, axis_name, split_axis=0, concat_axis=0, tiled=True)  54.8 us
    all_to_all x1, waiting for transfers between devices, gather_all(): lax.all_to_all(copies, axis_name, split_axis=0, concat_axis=0, tiled=True)  37 us
    all_to_all x1, waiting for transfers between devices, shards(): lax.all_to_all(send_rows, 'fsdp', split_axis=1, concat_axis=1, tiled=True)  34.7 us
    reduce_scatter x1, waiting for transfers between devices, shards(): lax.psum_scatter(partial_value.reshape(seq_count, own_rows, full_width).a...  33.9 us
    all_gather x1, waiting for transfers between devices, shards(): w_qkv = lax.all_gather(packed, 'fsdp', axis=0, tiled=True)  32.3 us
    all_to_all x1, blocking collectives, shards(): lax.all_to_all(back_rows, 'fsdp', split_axis=1, concat_axis=1, tiled=True)  23.9 us
    dot_general x1, matrix products, shards(): jnp.dot(normed, w_qkv, preferred_element_type=jnp.float32)  13.6 us
  transfers between devices with their start and end apart: 5, of which 5 were waited for; matrix products, arithmetic and copies ran while one was open for 14% of the time, Pallas kernels for 0%

profile of v9, /device:TPU:0, one launch (start us, length us, event | category | flops | bytes accessed | tf_op | source)
XLA Modules:
  0.0 383.6 jit_solution(11395040627469000064)
XLA Ops:
  6.5 0.0 all-gather.3.cloned.1.call-start
  6.5 1.4 dynamic_update_slice.9
  7.9 0.9 constant_dynamic-update-slice_fusion.1
  8.9 0.9 constant_dynamic-update-slice_fusion
  9.8 0.0 copy-start
  9.8 1.1 copy-done
  10.9 0.0 all-gather.3.cloned.1.call-update
  10.9 0.0 all-gather.5.cloned.1.call-start
  11.0 1.3 copy.44
  12.3 0.0 all-gather.5.cloned.1.call-update
  12.3 0.2 reduce_window_sum.11
  12.5 0.2 dynamic-slice_reduce_fusion
  12.8 0.1 and_select_fusion.3
  12.8 0.1 add.260
  12.9 0.1 add.261
  13.0 0.1 add.250
  13.1 0.1 add.253
  13.2 0.1 add.254
  13.3 0.1 add.247
  13.4 0.1 add.248
  13.4 0.1 lt.92
  13.5 0.1 lt.93
  13.6 0.3 select_reduce_fusion
  13.9 0.1 compare_select_fusion.3
  14.0 3.8 fusion.18
  17.8 2.4 copy.35
  20.2 7.1 %all-to-all-start = ((bf16[2,16,20,1024]{3,0,2,1:T(2,128)(2,1)}), bf16[2,16,20,1024]{3,0,2,1:T(2,128)(2,1)S(1)}, u32[]{:S(2)}, u32[]{:S(2)}) async-start(bf16[2,16,20,1024]{3,0,2,1:T(2,128)(2,1)} %bitcast), calls=%async_computation | async-start | bytes 2621440 | tf_op jit(solution)/shard_map/all_to_all | solution.py:71
  27.4 0.1 convert_reduce_fusion
  27.4 0.1 select_reduce_fusion.1
  27.6 34.7 %all-to-all-done = bf16[2,16,20,1024]{3,0,2,1:T(2,128)(2,1)S(1)} async-done(((bf16[2,16,20,1024]{3,0,2,1:T(2,128)(2,1)}), bf16[2,16,20,1024]{3,0,2,1:T(2,128)(2,1)S(1)}, u32[]{:S(2)}, u32[]{:S(2)}) %all-to-all-start) | async-done | bytes 1310752 | tf_op jit(solution)/shard_map/all_to_all | solution.py:71
  62.3 0.6 fusion.27
  62.9 0.5 broadcast_in_dim.62
  63.4 54.8 %all_to_all.20 = bf16[8,2,128,1024]{3,2,1,0:T(8,128)(2,1)S(1)} all-to-all(bf16[8,2,128,1024]{3,2,1,0:T(8,128)(2,1)S(1)} %broadcast_in_dim.62), channel_id=1, replica_groups=mesh['seq'=8,'fsdp'=16] {'seq'}, dimensions={0} | all-to-all | bytes 8388608 | tf_op jit(solution)/shard_map/all_to_all | solution.py:33
  118.2 2.3 copy.37
  120.6 6.3 %copy.54 = bf16[32,8,8,1024]{3,1,2,0:T(8,128)(2,1)} copy(bf16[32,8,8,1024]{3,2,1,0:T(8,128)(2,1)S(1)} %bitcast.98) | data formatting | bytes 8388608
  126.9 0.9 multiply_reduce_fusion
  127.8 32.3 %all-gather.3.cloned.1.call-done = bf16[8192,1280]{1,0:T(8,128)(2,1)} async-done(((bf16[512,1280]{1,0:T(8,128)(2,1)}), bf16[8192,1280]{1,0:T(8,128)(2,1)}) %all-gather.3.cloned.1.call-update) | async-done | bytes 20971536 | tf_op jit(solution)/shard_map/all_gather | solution.py:55
  160.1 13.6 %fusion.16 = bf16[256,1280]{1,0:T(8,128)(2,1)S(1)} fusion(bf16[8192,1280]{1,0:T(8,128)(2,1)} %all-gather.3.cloned.1.call-done, bf16[256,8192]{1,0:T(8,128)(2,1)} %bitcast.96, f32[8192]{0:T(1024)S(1)} %copy-done.6, f32[256]{0:T(256)S(1)} %rsqrt_bitcast_fusion), kind=kOutput, calls=%fused_computation.20 | convolution fusion | flops 5377425408 | bytes 25854976 | tf_op jit(solution)/shard_map/dot_general | solution.py:93
  173.7 0.0 copy-start.3
  173.7 1.6 broadcast_in_dim.64
  175.3 5.3 %all-to-all-start.2 = ((bf16[16,2,128,256]{3,2,1,0:T(8,128)(2,1)}), bf16[16,2,128,256]{3,2,1,0:T(8,128)(2,1)S(1)}, u32[]{:S(2)}, u32[]{:S(2)}) async-start(bf16[16,2,128,256]{3,2,1,0:T(8,128)(2,1)} %broadcast_in_dim.64), calls=%async_computation.2 | async-start | bytes 4194304 | tf_op jit(solution)/shard_map/all_to_all | solution.py:33
  180.6 0.3 reduce-scatter.2.cloned.1.call-start
  180.9 0.1 copy.39
  181.0 0.1 fusion.54
  181.1 0.2 broadcast_compare_fusion
  181.4 1.4 fusion.17
  182.8 1.9 copy.40
  184.7 0.1 slice_bitcast_fusion.6
  184.7 0.1 copy.55
  184.8 37.0 %all-to-all-done.2 = bf16[16,2,128,256]{3,2,1,0:T(8,128)(2,1)S(1)} async-done(((bf16[16,2,128,256]{3,2,1,0:T(8,128)(2,1)}), bf16[16,2,128,256]{3,2,1,0:T(8,128)(2,1)S(1)}, u32[]{:S(2)}, u32[]{:S(2)}) %all-to-all-start.2) | async-done | bytes 2097184 | tf_op jit(solution)/shard_map/all_to_all | solution.py:33
  221.8 0.1 copy.38
  221.9 2.7 fusion.2
  224.6 4.0 %fusion.3 = f32[2,8,128]{2,1,0:T(8,128)S(1)} fusion(f32[2,2048,128,8]{2,1,3,0:T(8,128)S(1)} %get-tuple-element.12, f32[2,8,128]{2,1,0:T(8,128)S(1)} %get-tuple-element.11, pred[2,128,2048]{1,2,0:T(8,128)(4,1)S(1)} %copy.40), kind=kLoop, calls=%fused_computation.5 | loop fusion | flops 20969472 | bytes 17317888 | tf_op jit(solution)/shard_map/reduce_sum | solution.py:120
  228.7 4.2 %divide_convert_fusion = bf16[2,128,1,8,128]{1,4,3,0,2:T(8,128)(2,1)S(1)} fusion(f32[2,2048,128,8]{2,1,3,0:T(8,128)S(1)} %get-tuple-element.12, f32[2,8,128]{2,1,0:T(8,128)S(1)} %get-tuple-element.11, pred[2,128,2048]{1,2,0:T(8,128)(4,1)S(1)} %copy.40, bf16[2,2048,256]{2,1,0:T(8,128)(2,1)S(1)} %bitcast.103, f32[2,128,8]{1,2,0:T(8,128)S(1)} %bitcast.110), kind=kOutput, calls=%fused_computation.37 | convolution fusion | flops 1095237632 | bytes 18890752 | tf_op jit(solution)/shard_map/skgqt,stkd->sqkgd/dot_general | solution.py:121
  232.9 62.5 %all-gather.5.cloned.1.call-done = bf16[8192,1024]{1,0:T(8,128)(2,1)} async-done(((bf16[512,1024]{1,0:T(8,128)(2,1)}), bf16[8192,1024]{1,0:T(8,128)(2,1)}) %all-gather.5.cloned.1.call-update) | async-done | bytes 16777232 | tf_op jit(solution)/shard_map/all_gather | solution.py:56
  295.5 9.7 %fusion.5 = bf16[2,128,8192]{2,1,0:T(8,128)(2,1)} fusion(bf16[2,128,1024]{1,2,0:T(8,128)(2,1)S(1)} %bitcast.112, bf16[8192,1024]{1,0:T(8,128)(2,1)} %all-gather.5.cloned.1.call-done), kind=kOutput, calls=%fused_computation.7 | convolution fusion | flops 4297064448 | bytes 21495808 | tf_op jit(solution)/shard_map/rk,nk->rn/dot_general | solution.py:132
  305.2 0.0 reduce-scatter.2.cloned.1.call-update
  305.2 0.7 copy-done.2
  305.9 3.4 fusion.71
  309.3 33.9 %reduce-scatter.2.cloned.1.call-done = bf16[2,128,1024]{2,1,0:T(8,128)(2,1)} async-done(((bf16[2,128,8192]{2,1,0:T(8,128)(2,1)}), bf16[2,128,1024]{2,1,0:T(8,128)(2,1)}) %reduce-scatter.2.cloned.1.call-update) | async-done | bytes 524304 | tf_op jit(solution)/shard_map/reduce_scatter | solution.py:135
  343.2 1.6 convolution_convert_fusion.1
  344.8 1.3 copy.46
  346.2 23.9 %all_to_all.21 = bf16[2,16,20,1024]{3,0,2,1:T(2,128)(2,1)S(1)} all-to-all(bf16[2,16,20,1024]{3,0,2,1:T(2,128)(2,1)S(1)} %bitcast.100), channel_id=1, replica_groups=mesh['seq'=8,'fsdp'=16] {'fsdp'}, dimensions={1} | all-to-all | bytes 2621440 | tf_op jit(solution)/shard_map/all_to_all | solution.py:151
  370.0 7.0 %convert_add_fusion = f32[2,1024,1024]{2,1,0:T(8,128)} fusion(bf16[2,1024,1024]{2,1,0:T(8,128)(2,1)} %param.10, s32[2,320]{1,0:T(2,128)S(1)} %get-tuple-element.10, bf16[2,320,1024]{2,0,1:T(2,128)(2,1)S(1)} %bitcast.105, s32[2,320]{1,0:T(2,128)S(1)} %get-tuple-element.9), kind=kOutput, calls=%fused_computation.11 | convolution fusion | flops 1767317504 | bytes 13898752 | tf_op jit(solution)/shard_map/skp,skc->spc/dot_general | solution.py:160
  (25 shorter events, 0.2 us)
Async XLA Ops:
  6.5 4.4 %copy-start.1 = (bf16[1024,512]{1,0:T(8,128)(2,1)S(1)}, bf16[1024,512]{1,0:T(8,128)(2,1)}, u32[]{:S(2)}) copy-start(bf16[1024,512]{1,0:T(8,128)(2,1)} %param.19) | copy-start | bytes 3145732
  6.5 5.8 %copy-start.4 = (s32[2,16]{1,0:T(2,128)S(1)}, s32[2,16]{1,0:T(2,128)}, u32[]{:S(2)}) copy-start(s32[2,16]{1,0:T(2,128)} %param.12) | copy-start | bytes 388
  6.5 7.1 %copy-start.5 = (s32[2,320]{1,0:T(2,128)S(1)}, s32[2,320]{1,0:T(2,128)}, u32[]{:S(2)}) copy-start(s32[2,320]{1,0:T(2,128)} %param.11) | copy-start | bytes 7684
  6.5 153.6 %all-gather.3.cloned.1.call-start = ((), (), s32[]{:S(2)}) async-start(), calls=%async_computation.5 | async-start | bytes 22282240 | tf_op jit(solution)/shard_map/all_gather | solution.py:55
  9.8 1.1 copy-start
  10.9 284.5 %all-gather.5.cloned.1.call-start = ((), (), s32[]{:S(2)}) async-start(), calls=%async_computation.6 | async-start | bytes 17825792 | tf_op jit(solution)/shard_map/all_gather | solution.py:56
  20.2 42.1 %all-to-all-start = ((bf16[2,16,20,1024]{3,0,2,1:T(2,128)(2,1)}), bf16[2,16,20,1024]{3,0,2,1:T(2,128)(2,1)S(1)}, u32[]{:S(2)}, u32[]{:S(2)}) async-start(bf16[2,16,20,1024]{3,0,2,1:T(2,128)(2,1)} %bitcast), calls=%async_computation | async-start | bytes 2621440 | tf_op jit(solution)/shard_map/all_to_all | solution.py:71
  126.9 33.2 %copy-start.6 = (f32[8192]{0:T(1024)S(1)}, f32[8192]{0:T(1024)}, u32[]{:S(2)}) copy-start(f32[8192]{0:T(1024)} %param.15) | copy-start | bytes 98308
  173.7 7.2 %copy-start.3 = (s32[2,16,16]{2,1,0:T(8,128)S(1)}, s32[2,16,16]{2,1,0:T(8,128)}, u32[]{:S(2)}) copy-start(s32[2,16,16]{2,1,0:T(8,128)} %param.13) | copy-start | bytes 6148
  175.3 46.5 %all-to-all-start.2 = ((bf16[16,2,128,256]{3,2,1,0:T(8,128)(2,1)}), bf16[16,2,128,256]{3,2,1,0:T(8,128)(2,1)S(1)}, u32[]{:S(2)}, u32[]{:S(2)}) async-start(bf16[16,2,128,256]{3,2,1,0:T(8,128)(2,1)} %broadcast_in_dim.64), calls=%async_computation.2 | async-start | bytes 4194304 | tf_op jit(solution)/shard_map/all_to_all | solution.py:33
  180.6 162.6 %reduce-scatter.2.cloned.1.call-start = ((), (), s32[]{:S(2)}) async-start(), calls=%async_computation.7 | async-start | bytes 4718592 | tf_op jit(solution)/shard_map/reduce_scatter | solution.py:135
  305.2 0.7 copy-start.2
Sparse Core Ops, SparseCore 0:
  11.0 149.0 all-gather.2
  162.3 133.1 all-gather.4
  305.4 37.7 reduce-scatter.1
